TPU v7x, 256 devices: a whole 4x4x8 slice. The times are simulated.
256 devices in a mesh: dp: 32 (over x, y, core), mp: 8 (over z).
Axes of the slice: x: 4, y: 4, z: 8, core: 2. Of those that a mesh axis runs over, the one named last changes fastest.
Arguments:
- weight: bfloat16 [1024, 128, 128], P(('dp', 'mp')), may hold values from -6 to 6
- moment_one: float32 [1024, 128, 128], P(('dp', 'mp')), may hold values from -1.8 to 1.8
- moment_two: float32 [1024, 128, 128], P(('dp', 'mp')), may hold values from 0.01 to 1
- block_row: int32 [1024], P(('dp', 'mp')), may hold values from 0 to 63, as said below
- block_col: int32 [1024], P(('dp', 'mp')), may hold values from 0 to 27
- dest_slot: int32 [1024], P(('dp', 'mp')), may hold values from -1 to 127, as said below
- tokens: bfloat16 [4096, 8192], P('dp', 'mp'), may hold values from -6 to 6
- upstream: bfloat16 [4096, 28672], P('dp', 'mp'), may hold values from -6 to 6
Outputs:
- new_weight: bfloat16 [1024, 128, 128], P(('dp', 'mp'))
- new_first: float32 [1024, 128, 128], P(('dp', 'mp'))
- new_second: float32 [1024, 128, 128], P(('dp', 'mp'))
- hidden_out: bfloat16 [4096, 28672], P('dp', 'mp')
- input_grad: bfloat16 [4096, 8192], P('dp', 'mp')
Inputs may be any that keep to these rules, and one draw needn't show every extreme that they name: Within one tensor slice the pairs (block_row, block_col) are distinct. `dest_slot`: within one tensor slice the non-negative values are distinct; slots d * 4 to (d + 1) * 4 - 1 belong to dp index d, and a block held by dp index d goes to d - 1, d or d + 1; at most 2 blocks of one device go to each neighbour, and in every slice some pair of neighbours exchanges exactly 2 blocks each way.
All inputs are finite; a program needn't handle non-finite values.
Results may differ from a plain program's by a relative error of at most 0.0055.
Values may be sent and summed in bfloat16 or wider, within the bound.
A program may use at most 128 MiB of HBM per device.

v0:
```python
import math

import jax
import jax.numpy as jnp
from jax import lax
from jax.sharding import PartitionSpec as P

D = 8192


learn_rate = 0.02
beta_first = 0.9
beta_second = 0.95
epsilon = 1e-08
highest = lax.Precision.HIGHEST


def with_halo(shard, sides, width):
    for axis, dim in sides:
        size, length = (lax.axis_size(axis), shard.shape[dim])
        up = [(i, (i + 1) % size) for i in range(size - 1)]
        down = [(j, i) for i, j in up]
        last = lax.slice_in_dim(shard, length - width, length, axis=dim)
        initial = lax.slice_in_dim(shard, 0, width, axis=dim)
        before = lax.ppermute(last, axis, up)
        after = lax.ppermute(initial, axis, down)
        shard = jnp.concatenate([before, shard, after], axis=dim)
    return shard


def adam_update(gradient, weights, first_moment, second_moment):
    first_new = beta_first * first_moment + (1.0 - beta_first) * gradient
    second_new = beta_second * second_moment + (1.0 - beta_second) * gradient * gradient
    stepped = weights - learn_rate * first_new / (jnp.sqrt(second_new) + epsilon)
    return (stepped, first_new, second_new)


def moving_plan(dest_part, goal, kept_dev, half_slots):
    chosen = (dest_part >= 0) & (dest_part // kept_dev == goal)
    order_rank = jnp.cumsum(chosen.astype(jnp.int32)) - 1
    select = (
        (order_rank[None, :] == jnp.arange(half_slots, dtype=jnp.int32)[:, None]) & chosen[None, :]
    ).astype(jnp.float32)
    offsets = (
        jnp.dot(select, (dest_part % kept_dev + 1).astype(jnp.float32), precision=highest) - 1.0
    )
    return (select, offsets)


def relocate(stacked, all_dest):
    kept_dev = stacked.shape[0]
    half_slots = kept_dev // 2
    own_index = lax.axis_index("dp")
    last_index = lax.axis_size("dp") - 1
    own_dest = lax.dynamic_slice_in_dim(all_dest, own_index * kept_dev, kept_dev)
    left_dest = lax.dynamic_slice_in_dim(
        all_dest, jnp.maximum(own_index - 1, 0) * kept_dev, kept_dev
    )
    right_dest = lax.dynamic_slice_in_dim(
        all_dest, jnp.minimum(own_index + 1, last_index) * kept_dev, kept_dev
    )
    send_left, unused_left = moving_plan(own_dest, own_index - 1, kept_dev, half_slots)
    send_right, unused_right = moving_plan(own_dest, own_index + 1, kept_dev, half_slots)
    outgoing = jnp.dot(jnp.concatenate([send_left, send_right], axis=0), stacked, precision=highest)
    padded = with_halo(outgoing.astype(jnp.bfloat16), (("dp", 0),), half_slots).astype(
        outgoing.dtype
    )
    from_left = padded[:half_slots]
    from_right = padded[3 * half_slots :]
    unused_one, left_offsets = moving_plan(left_dest, own_index, kept_dev, half_slots)
    unused_two, right_offsets = moving_plan(right_dest, own_index, kept_dev, half_slots)
    left_offsets = jnp.where(own_index > 0, left_offsets, -1.0)
    right_offsets = jnp.where(own_index < last_index, right_offsets, -1.0)
    staying = (own_dest >= 0) & (own_dest // kept_dev == own_index)
    stay_offsets = jnp.where(staying, own_dest % kept_dev, -1).astype(jnp.float32)
    places = jnp.concatenate([stay_offsets, left_offsets, right_offsets])
    slot_hot = (jnp.arange(kept_dev, dtype=jnp.float32)[:, None] == places[None, :]).astype(
        jnp.float32
    )
    return jnp.dot(
        slot_hot, jnp.concatenate([stacked, from_left, from_right], axis=0), precision=highest
    )


def body(weight, moment_one, moment_two, block_row, block_col, dest_slot, tokens, upstream):
    kept_dev = weight.shape[0]
    block_side = weight.shape[1]
    flat_size = block_side * block_side
    grad_scale = 1.0 / math.sqrt(D)
    features = lax.all_gather(tokens, "mp", axis=1, tiled=True)
    all_weight, all_rows, all_cols, all_dest = (
        lax.all_gather(weight, "dp", axis=0, tiled=True),
        lax.all_gather(block_row, "dp", axis=0, tiled=True),
        lax.all_gather(block_col, "dp", axis=0, tiled=True),
        lax.all_gather(dest_slot, "dp", axis=0, tiled=True),
    )
    token_rows = features.shape[0]
    block_rows = features.shape[1] // block_side
    block_cols = upstream.shape[1] // block_side
    x_blocks = jnp.take(features.reshape(token_rows, block_rows, block_side), all_rows, axis=1)
    d_blocks = jnp.take(upstream.reshape(token_rows, block_cols, block_side), all_cols, axis=1)
    forward = jnp.einsum("tbk,bkj->btj", x_blocks, all_weight, preferred_element_type=jnp.float32)
    col_sums = jax.ops.segment_sum(forward, all_cols, num_segments=block_cols)
    hidden_out = (
        (jnp.swapaxes(col_sums, 0, 1) * grad_scale)
        .reshape(token_rows, block_cols * block_side)
        .astype(jnp.bfloat16)
    )
    backward = jnp.einsum("tbj,bkj->btk", d_blocks, all_weight, preferred_element_type=jnp.float32)
    row_sums = jax.ops.segment_sum(backward, all_rows, num_segments=block_rows)
    partial_in = (jnp.swapaxes(row_sums, 0, 1) * grad_scale).reshape(
        token_rows, block_rows * block_side
    )
    input_grad = lax.psum_scatter(partial_in, "mp", scatter_dimension=1, tiled=True).astype(
        jnp.bfloat16
    )
    old_weight = weight.reshape(kept_dev, flat_size).astype(jnp.float32)
    old_first = moment_one.reshape(kept_dev, flat_size)
    old_second = moment_two.reshape(kept_dev, flat_size)
    gradient = (
        lax.psum_scatter(
            (
                jnp.einsum("tbk,tbj->bkj", x_blocks, d_blocks, preferred_element_type=jnp.float32)
                * grad_scale
            ).astype(jnp.bfloat16),
            "dp",
            scatter_dimension=0,
            tiled=True,
        )
        .astype(jnp.float32)
        .reshape(kept_dev, flat_size)
    )
    held_weight, held_first, held_second = adam_update(gradient, old_weight, old_first, old_second)
    moved = relocate(jnp.concatenate([held_weight, held_first, held_second], axis=1), all_dest)
    stepped = moved[:, :flat_size]
    first_new = moved[:, flat_size : 2 * flat_size]
    second_new = moved[:, 2 * flat_size :]
    new_weight = stepped.astype(jnp.bfloat16).reshape(kept_dev, block_side, block_side)
    new_first = first_new.reshape(kept_dev, block_side, block_side)
    new_second = second_new.reshape(kept_dev, block_side, block_side)
    return (new_weight, new_first, new_second, hidden_out, input_grad)


def solution(mesh):
    return jax.shard_map(
        body,
        mesh=mesh,
        in_specs=(
            P(("dp", "mp"), None, None),
            P(("dp", "mp"), None, None),
            P(("dp", "mp"), None, None),
            P(("dp", "mp")),
            P(("dp", "mp")),
            P(("dp", "mp")),
            P("dp", "mp"),
            P("dp", "mp"),
        ),
        out_specs=(
            P(("dp", "mp"), None, None),
            P(("dp", "mp"), None, None),
            P(("dp", "mp"), None, None),
            P("dp", "mp"),
            P("dp", "mp"),
        ),
        check_vma=False,
    )
```

profile of v0, /device:TPU:2, one launch (start us, length us, event | category | flops | bytes accessed | tf_op | source)
XLA Modules:
  0.0 265.4 jit_solution(6325529828140879658)
XLA Ops:
  7.2 0.0 copy-start.10
  7.2 0.0 all-gather.3.cloned.1.call-start
  7.3 1.8 copy.28
  9.0 0.0 all-gather.3.cloned.1.call-update
  9.1 0.0 all-gather.5.cloned.1.call-start
  9.1 0.7 all-gather.5.cloned.1.call-update
  9.8 0.0 reduce-scatter.3.cloned.1.call-start
  9.9 1.6 copy.30
  11.4 0.6 copy.31
  12.1 0.6 dynamic-slice
  13.4 0.2 dynamic-update-slice.1
  13.6 0.2 dynamic-update-slice.2
  13.8 0.2 dynamic-update-slice
  14.1 15.6 %all-reduce.3 = (s32[128]{0:T(128)S(1)}, s32[128]{0:T(128)S(1)}, s32[128]{0:T(128)S(1)}) all-reduce(s32[128]{0:T(128)S(1)} %dynamic-update-slice.1, s32[128]{0:T(128)S(1)} %dynamic-update-slice.2, s32[128]{0:T(128)S(1)} %dynamic-update-slice), channel_id=1, replica_groups=mesh['dp'=32,'mp'=8] {'dp'}, use_global_device_ids=true, to_apply=%add.1 | all-reduce | flops 384 | bytes 3072
  29.7 3.1 %gather_fusion.1 = bf16[128,128,128]{2,1,0:T(8,128)(2,1)} fusion(bf16[128,28,128]{2,0,1:T(8,128)(2,1)S(1)} %copy.31, s32[1024]{0:T(1024)S(1)} %pad_clamp_fusion), kind=kCustom, calls=%fused_computation.1 | custom fusion | bytes 8389120 | tf_op jit(solution)/shard_map/jit(_take)/gather | solution.py:101
  32.8 21.4 %all-gather.3.cloned.1.call-done = bf16[128,8192]{0,1:T(8,128)(2,1)} async-done(((bf16[128,1024]{0,1:T(8,128)(2,1)}), bf16[128,8192]{0,1:T(8,128)(2,1)}) %all-gather.3.cloned.1.call-update) | async-done | bytes 2097168 | tf_op jit(solution)/shard_map/all_gather | solution.py:90
  54.2 3.2 %copy.29 = bf16[128,64,128]{2,0,1:T(8,128)(2,1)S(1)} copy(bf16[128,64,128]{0,2,1:T(8,128)(2,1)} %bitcast.100) | data formatting | bytes 4194304 | tf_op jit(solution)/shard_map/reshape | solution.py:100
  57.4 3.0 %gather_fusion = bf16[128,128,128]{2,1,0:T(8,128)(2,1)} fusion(bf16[128,64,128]{2,0,1:T(8,128)(2,1)S(1)} %copy.29, s32[1024]{0:T(1024)S(1)} %pad_clamp_fusion.1), kind=kCustom, calls=%fused_computation | custom fusion | bytes 8389120 | tf_op jit(solution)/shard_map/jit(_take)/gather | solution.py:100
  60.5 7.5 %multiply_convert_fusion = bf16[128,128,128]{2,1,0:T(8,128)(2,1)} fusion(bf16[128,128,128]{2,1,0:T(8,128)(2,1)} %gather_fusion, pred[128]{0:T(512)(128)(4,1)S(1)} %get-tuple-element.48, bf16[128,128,128]{2,1,0:T(8,128)(2,1)} %gather_fusion.1, pred[128]{0:T(512)(128)(4,1)S(1)} %get-tuple-element.47), kind=kOutput, calls=%fused_computation.5 | convolution fusion | flops 545259520 | bytes 12583168 | tf_op jit(solution)/shard_map/tbk,tbj->bkj/dot_general | solution.py:123
  67.9 0.0 reduce-scatter.3.cloned.1.call-update
  68.0 0.2 reduce-scatter.5.cloned.1.call-start
  68.2 0.1 fusion.53
  68.3 0.2 reduce-window.35
  68.5 0.2 reduce-window.34
  68.7 0.1 convert_bitcast_fusion.5
  68.8 0.2 reduce-window.33
  68.9 0.2 reduce-window.32
  69.1 0.2 fusion.24
  69.3 0.2 fusion.22
  69.5 0.1 pad_maximum_fusion.2
  69.8 36.4 %all-gather.5.cloned.1.call-done = bf16[128,128,128]{2,1,0:T(8,128)(2,1)} async-done(((bf16[4,128,128]{2,1,0:T(8,128)(2,1)}), bf16[128,128,128]{2,1,0:T(8,128)(2,1)}) %all-gather.5.cloned.1.call-update) | async-done | bytes 4194320 | tf_op jit(solution)/shard_map/all_gather | solution.py:92
  106.1 9.8 %fusion = f32[128,128,128]{2,1,0:T(8,128)} fusion(bf16[128,128,128]{2,1,0:T(8,128)(2,1)} %all-gather.5.cloned.1.call-done, bf16[128,128,128]{2,1,0:T(8,128)(2,1)} %gather_fusion.1, pred[128]{0:T(512)(128)(4,1)S(1)} %get-tuple-element.47), kind=kOutput, calls=%fused_computation.6 | convolution fusion | flops 538968064 | bytes 16777344 | tf_op jit(solution)/shard_map/tbj,bkj->btk/dot_general | solution.py:109
  115.9 2.5 broadcast_in_dim.60
  118.4 27.0 %scatter_fusion.1 = f32[64,128,128]{2,1,0:T(8,128)} fusion(f32[64,128,128]{2,1,0:T(8,128)} %broadcast_in_dim.60, s32[128]{0:T(128)S(1)} %get-tuple-element.20, f32[128,128,128]{2,1,0:T(8,128)} %fusion), kind=kCustom, calls=%fused_computation.3 | custom fusion | flops 2097152 | bytes 25166336 | tf_op jit(solution)/shard_map/scatter-add | solution.py:110
  145.4 5.0 %multiply_bitcast_fusion = f32[128,64,128]{2,0,1:T(8,128)} fusion(f32[64,128,128]{2,1,0:T(8,128)} %scatter_fusion.1), kind=kLoop, calls=%fused_computation.13 | loop fusion | flops 1048576 | bytes 8388608 | tf_op jit(solution)/shard_map/mul | solution.py:111
  150.4 5.6 %copy.34 = f32[128,64,128]{0,2,1:T(8,128)} copy(f32[128,64,128]{2,0,1:T(8,128)} %multiply_bitcast_fusion) | data formatting | bytes 8388608 | tf_op jit(solution)/shard_map/mul | solution.py:111
  156.0 8.0 %fusion.4 = f32[128,128,128]{2,1,0:T(8,128)} fusion(bf16[128,128,128]{2,1,0:T(8,128)(2,1)} %all-gather.5.cloned.1.call-done, bf16[128,128,128]{2,1,0:T(8,128)(2,1)} %gather_fusion, pred[128]{0:T(512)(128)(4,1)S(1)} %get-tuple-element.48), kind=kOutput, calls=%fused_computation.10 | convolution fusion | flops 538968064 | bytes 16777344 | tf_op jit(solution)/shard_map/tbk,bkj->btj/dot_general | solution.py:102
  164.1 0.2 broadcast_in_dim.58
  164.2 17.1 %scatter_fusion = f32[28,128,128]{2,1,0:T(8,128)S(1)} fusion(f32[28,128,128]{2,1,0:T(8,128)S(1)} %broadcast_in_dim.58, s32[128]{0:T(128)S(1)} %get-tuple-element.21, f32[128,128,128]{2,1,0:T(8,128)} %fusion.4), kind=kCustom, calls=%fused_computation.2 | custom fusion | flops 2097152 | bytes 25166336 | tf_op jit(solution)/shard_map/scatter-add | solution.py:103
  181.4 0.0 reduce-scatter.5.cloned.1.call-update
  181.4 18.1 %reduce-scatter.3.cloned.1.call-done = bf16[4,128,128]{2,1,0:T(8,128)(2,1)} async-done(((bf16[128,128,128]{2,1,0:T(8,128)(2,1)}), bf16[4,128,128]{2,1,0:T(8,128)(2,1)}) %reduce-scatter.3.cloned.1.call-update) | async-done | bytes 131088 | tf_op jit(solution)/shard_map/reduce_scatter | solution.py:121
  199.5 0.9 convert_bitcast_fusion
  200.4 0.8 bitcast_subtract_fusion
  201.2 0.0 copy-start.1
  201.2 0.0 copy-start.3
  201.2 0.9 convolution_convert_fusion
  202.2 1.0 fusion.74
  203.2 1.9 collective-permute-start.1
  205.1 2.6 collective-permute-start
  207.8 0.3 fusion.25
  208.0 0.0 copy-start.2
  208.1 0.0 copy-start.4
  208.1 0.6 copy.33
  208.7 1.3 copy.35
  210.0 0.0 collective-permute-done.1
  210.0 4.6 %collective-permute-done = bf16[2,49152]{1,0:T(2,128)(2,1)} collective-permute-done((bf16[2,49152]{1,0:T(2,128)(2,1)}, bf16[2,49152]{1,0:T(2,128)(2,1)}, u32[]{:S(2)}, u32[]{:S(2)}) %collective-permute-start) | collective-permute-done | bytes 196640 | tf_op jit(solution)/shard_map/ppermute | solution.py:25
  214.6 2.4 maximum_convert_fusion
  217.0 1.3 fusion.11
  218.3 0.7 copy.59
  219.0 0.7 copy.58
  219.7 0.7 copy.57
  220.4 36.5 %reduce-scatter.5.cloned.1.call-done = f32[128,1024]{0,1:T(8,128)} async-done(((f32[128,8192]{0,1:T(8,128)}), f32[128,1024]{0,1:T(8,128)}) %reduce-scatter.5.cloned.1.call-update) | async-done | bytes 524304 | tf_op jit(solution)/shard_map/reduce_scatter | solution.py:114
  257.0 1.1 convert_element_type.58
  258.1 0.9 copy.36
  (35 shorter events, 0.3 us)
Async XLA Ops:
  7.2 4.9 %copy-start.10 = (u32[256]{0:T(256)S(1)}, u32[256]{0:T(256)}, u32[]{:S(2)}) copy-start(u32[256]{0:T(256)} %constant.143) | copy-start | bytes 3076
  7.2 6.2 %copy-start.7 = (s32[4]{0:T(128)S(1)}, s32[4]{0:T(128)}, u32[]{:S(2)}) copy-start(s32[4]{0:T(128)} %param.11) | copy-start | bytes 52
  7.2 6.4 %copy-start.8 = (s32[4]{0:T(128)S(1)}, s32[4]{0:T(128)}, u32[]{:S(2)}) copy-start(s32[4]{0:T(128)} %param.12) | copy-start | bytes 52
  7.2 6.6 %copy-start.9 = (s32[4]{0:T(128)S(1)}, s32[4]{0:T(128)}, u32[]{:S(2)}) copy-start(s32[4]{0:T(128)} %param.13) | copy-start | bytes 52
  7.2 47.0 %all-gather.3.cloned.1.call-start = ((), (), s32[]{:S(2)}) async-start(), calls=%async_computation.2 | async-start | bytes 2359296 | tf_op jit(solution)/shard_map/all_gather | solution.py:90
  9.1 97.1 %all-gather.5.cloned.1.call-start = ((), (), s32[]{:S(2)}) async-start(), calls=%async_computation.4 | async-start | bytes 4325376 | tf_op jit(solution)/shard_map/all_gather | solution.py:92
  9.8 189.7 %reduce-scatter.3.cloned.1.call-start = ((), (), s32[]{:S(2)}) async-start(), calls=%async_computation.3 | async-start | bytes 4325376 | tf_op jit(solution)/shard_map/reduce_scatter | solution.py:121
  67.9 1.7 copy-start
  67.9 1.7 copy-start.5
  67.9 1.8 copy-start.6
  68.0 189.0 %reduce-scatter.5.cloned.1.call-start = ((), (), s32[]{:S(2)}) async-start(), calls=%async_computation.5 | async-start | bytes 4718592 | tf_op jit(solution)/shard_map/reduce_scatter | solution.py:114
  201.2 3.9 %copy-start.1 = (f32[4,16384]{1,0:T(4,128)}, f32[4,16384]{1,0:T(4,128)S(1)}, u32[]{:S(2)}) copy-start(f32[4,16384]{1,0:T(4,128)S(1)} %get-tuple-element.35) | copy-start | bytes 786436
  201.2 3.9 %copy-start.3 = (f32[4,16384]{1,0:T(4,128)}, f32[4,16384]{1,0:T(4,128)S(1)}, u32[]{:S(2)}) copy-start(f32[4,16384]{1,0:T(4,128)S(1)} %get-tuple-element.36) | copy-start | bytes 786436
  203.2 6.8 %collective-permute-start.1 = (bf16[2,49152]{1,0:T(2,128)(2,1)}, bf16[2,49152]{1,0:T(2,128)(2,1)}, u32[]{:S(2)}, u32[]{:S(2)}) collective-permute-start(bf16[2,49152]{1,0:T(2,128)(2,1)} %get-tuple-element.42), channel_id=1, source_target_pairs={{8,0},{16,8},{24,16},{32,24},{40,32},{48,40},{56,48},{64,56},{72,6... | collective-permute-start | bytes 589832 | tf_op jit(solution)/shard_map/ppermute | solution.py:26
  205.1 9.4 %collective-permute-start = (bf16[2,49152]{1,0:T(2,128)(2,1)}, bf16[2,49152]{1,0:T(2,128)(2,1)}, u32[]{:S(2)}, u32[]{:S(2)}) collective-permute-start(bf16[2,49152]{1,0:T(2,128)(2,1)} %get-tuple-element.41), channel_id=1, source_target_pairs={{0,8},{8,16},{16,24},{24,32},{32,40},{40,48},{48,56},{56,64},{64,7... | collective-permute-start | bytes 589832 | tf_op jit(solution)/shard_map/ppermute | solution.py:25
  208.0 8.9 %copy-start.2 = (f32[4,16384]{1,0:T(4,128)S(1)}, f32[4,16384]{1,0:T(4,128)}, u32[]{:S(2)}) copy-start(f32[4,16384]{1,0:T(4,128)} %copy-done.1) | copy-start | bytes 786436
  208.1 8.9 %copy-start.4 = (f32[4,16384]{1,0:T(4,128)S(1)}, f32[4,16384]{1,0:T(4,128)}, u32[]{:S(2)}) copy-start(f32[4,16384]{1,0:T(4,128)} %copy-done.3) | copy-start | bytes 786436
Sparse Core Ops, SparseCore 0:
  10.4 43.7 all-gather.2
  56.8 49.3 all-gather.4
  110.1 89.3 reduce-scatter.2
  201.9 55.0 reduce-scatter.4
where the time goes:
time: 267 us; the launch traced here: 265 us
  waiting for transfers between devices  118 us (44%)
  other arithmetic  55.7 us (21%)
  local copies, waits for them, and re-layouts  28.9 us (11%)
  matrix products  27.8 us (10%)
  blocking collectives  15.6 us (6%)
  between operations  14.8 us (6%)
  starting transfers between devices  4.88 us (2%)
    reduce_scatter x1, waiting for transfers between devices, body(): lax.psum_scatter(partial_in, 'mp', scatter_dimension=1, tiled=True)  36.5 us
    all_gather x1, waiting for transfers between devices, body(): lax.all_gather(weight, 'dp', axis=0, tiled=True)  36.4 us
    scatter-add x1, other arithmetic, body(): row_sums = jax.ops.segment_sum(backward, all_rows, num_segments=block_rows)  27 us
    all_gather x1, waiting for transfers between devices, body(): features = lax.all_gather(tokens, 'mp', axis=1, tiled=True)  21.4 us
    reduce_scatter x1, waiting for transfers between devices, body(): lax.psum_scatter((jnp.einsum('tbk,tbj->bkj', x_blocks, d_blocks, preferre...  18.1 us
    scatter-add x1, other arithmetic, body(): col_sums = jax.ops.segment_sum(forward, all_cols, num_segments=block_cols)  17.1 us
    unnamed x1, blocking collectives  15.6 us
    dot_general x1, matrix products, body(): jnp.einsum('tbj,bkj->btk', d_blocks, all_weight, preferred_element_type=j...  9.78 us
  transfers between devices with their start and end apart: 6, of which 5 were waited for; matrix products, arithmetic and copies ran while one was open for 41% of the time, Pallas kernels for 0%

commit v1 on v0

v1 whole, which is shorter than its diff:
```python
import math

import jax
import jax.numpy as jnp
from jax import lax
from jax.experimental import pallas as pl
from jax.experimental.pallas import tpu as pltpu
from jax.sharding import PartitionSpec as P

D = 8192
BS = 128
SCALE = 1.0 / math.sqrt(D)
LEARN = 0.02
B1 = 0.9
B2 = 0.95
EPS = 1e-08
NSEM = 128
MESH = pl.DeviceIdType.MESH

F32 = jnp.float32
BF16 = jnp.bfloat16
I32 = jnp.int32

UP = [(1, 0), (2, 1), (2, 0), (3, 1), (3, 0), (4, 1), (4, 0)]
DN = [(1, 1), (2, 0), (2, 1), (3, 0), (3, 1), (4, 0), (4, 1)]


def kernel(
    brow, bcol, bdst, weight, m1_in, m2_in, tokens, upstream,
    new_w, new_1, new_2, hidden, in_grad,
    x_all, w_all, meta, d_all, mom1, mom2, seg_b, seg_f, tab_v, tab,
    g_out, g_in, g_own, recv1, q_sum, recv2, zsend, zrecv,
    lsem, ssem, rsem,
):
    dp = lax.axis_index("dp")
    z = lax.axis_index("mp")
    c = lax.rem(dp, 2)
    y = lax.rem(dp // 2, 4)
    x = dp // 8

    def dev(xx, yy, cc, zz):
        return {"dp": (xx * 4 + yy) * 2 + cc, "mp": zz}

    def m4(v):
        return lax.rem(v + 8, 4)

    def m8(v):
        return lax.rem(v + 16, 8)

    zup, zdn = dev(x, y, c, m8(z + 1)), dev(x, y, c, m8(z - 1))
    partner = dev(x, y, 1 - c, z)
    left = {"dp": lax.rem(dp + 31, 32), "mp": z}
    right = {"dp": lax.rem(dp + 1, 32), "mp": z}
    xp, xm = dev(m4(x + 1), y, c, z), dev(m4(x - 1), y, c, z)
    yp, ym = dev(x, m4(y + 1), c, z), dev(x, m4(y - 1), c, z)

    def plus(h):
        return xp if h == 0 else yp

    def minus(h):
        return xm if h == 0 else ym

    counter = [0]
    pending = []

    def send(src, dst, device):
        i = counter[0]
        counter[0] += 1
        cp = pltpu.make_async_remote_copy(
            src_ref=src, dst_ref=dst, send_sem=ssem.at[i], recv_sem=rsem.at[i],
            device_id=device, device_id_type=MESH,
        )
        cp.start()
        pending.append(cp)
        return i, device

    def arrive(tag, region):
        i, device = tag
        pltpu.make_async_remote_copy(
            src_ref=region, dst_ref=region, send_sem=ssem.at[i], recv_sem=rsem.at[i],
            device_id=device, device_id_type=MESH,
        ).wait_recv()

    lcount = [0]

    def local(src, dst):
        i = lcount[0]
        lcount[0] += 1
        cp = pltpu.make_async_copy(src, dst, lsem.at[i])
        cp.start()
        return cp

    tok_cp = [local(tokens.at[:, pl.ds(i * BS, BS)], x_all.at[z * 8 + i]) for i in range(8)]
    w_cp = [local(weight.at[pl.ds(2 * h, 2)], w_all.at[x, y, c, h]) for h in range(2)]
    mom_cp = [local(m1_in, mom1.at[1]), local(m2_in, mom2.at[1])]
    d_cp = [local(upstream.at[:, pl.ds(i * BS, BS)], d_all.at[i]) for i in range(28)]

    sub8 = lax.broadcasted_iota(I32, (8, BS), 0)
    lane8 = lax.broadcasted_iota(I32, (8, BS), 1)
    own_meta = jnp.zeros((8, BS), I32)
    for j in range(4):
        at = lane8 == dp * 4 + j
        for r, ref in enumerate((brow, bcol, bdst)):
            own_meta = own_meta + jnp.where(at & (sub8 == r), ref[j], 0)
    meta[x, y, c] = own_meta

    off = {"dp": lax.rem(dp + 31 + 2 * c, 32), "mp": z}
    barrier = pltpu.get_barrier_semaphore()
    for peer in (zup, zdn, partner, off, xp, xm, yp, ym):
        pl.semaphore_signal(barrier, inc=1, device_id=peer, device_id_type=MESH)
    pl.semaphore_wait(barrier, 8)

    def xs(level, h):
        return x_all.at[pl.ds(level * 8 + h * 4, 4)]

    zt = {0: {}, 1: {}}

    def z_send(dirn, i):
        k, h = divmod(i, 2)
        if i == 6:
            h = dirn
        level = m8(z - k) if dirn == 0 else m8(z + k)
        zt[dirn][i] = send(xs(level, h), xs(level, h), zup if dirn == 0 else zdn)

    def z_wait(dirn, i):
        k, h = divmod(i, 2)
        if i == 6:
            h = dirn
        level = m8(z - k - 1) if dirn == 0 else m8(z + k + 1)
        arrive(zt[dirn][i], xs(level, h))

    def z_event(i):
        for dirn in (0, 1):
            z_wait(dirn, i)
            if i + 2 < 6:
                z_send(dirn, i + 2)
            elif i + 2 == 6 + dirn:
                z_send(dirn, 6)

    for cp in w_cp:
        cp.wait()
    mt = [send(meta.at[x, y, c], meta.at[x, y, c], d) for d in (xp, xm)]

    def w1(h, delta):
        return (m4(x + delta), y, c, h) if h == 0 else (x, m4(y + delta), c, h)

    w1t = {}
    for h in (0, 1):
        own = w_all.at[w1(h, 0)]
        w1t[h, 0] = send(own, own, plus(h))
        w1t[h, 1] = send(own, own, minus(h))
    for cp in tok_cp:
        cp.wait()
    for i in (0, 1):
        z_send(0, i)
        z_send(1, i)

    arrive(mt[0], meta.at[m4(x - 1), y, c])
    mt2 = send(meta.at[m4(x - 1), y, c], meta.at[m4(x - 1), y, c], xp)
    arrive(mt[1], meta.at[m4(x + 1), y, c])

    w1f = {}
    for h in (0, 1):
        arrive(w1t[h, 0], w_all.at[w1(h, -1)])
        r = w_all.at[w1(h, -1) + (0,)]
        w1f[h, 0] = send(r, r, plus(h))
        arrive(w1t[h, 1], w_all.at[w1(h, 1)])
        r = w_all.at[w1(h, 1) + (1,)]
        w1f[h, 1] = send(r, r, minus(h))
    arrive(mt2, meta.at[m4(x - 2), y, c])
    mt3 = [send(meta.at[:, y, c], meta.at[:, y, c], d) for d in (yp, ym)]
    z_event(0)
    for h in (0, 1):
        arrive(w1f[h, 0], w_all.at[w1(h, -2) + (0,)])
        arrive(w1f[h, 1], w_all.at[w1(h, 2) + (1,)])

    def w2(h, delta, cc):
        if h == 0:
            return (slice(None), m4(y + delta), cc, 0)
        return (m4(x + delta), slice(None), cc, 1)

    w2t = {}
    wpt = {}
    for h in (0, 1):
        own = w_all.at[w2(h, 0, c)]
        w2t[h, 0] = send(own, own, plus(1 - h))
        w2t[h, 1] = send(own, own, minus(1 - h))
    for h in (0, 1):
        own = w_all.at[w2(h, 0, c)]
        wpt[h, 0] = send(own, own, partner)
    arrive(mt3[0], meta.at[:, m4(y - 1), c])
    mt4 = send(meta.at[:, m4(y - 1), c], meta.at[:, m4(y - 1), c], yp)
    arrive(mt3[1], meta.at[:, m4(y + 1), c])
    z_event(1)
    arrive(mt4, meta.at[:, m4(y - 2), c])
    mt5 = send(meta.at[:, :, c], meta.at[:, :, c], partner)

    for cp in mom_cp:
        cp.wait()
    mom_t = []
    for ref in (mom1, mom2):
        mom_t.append((send(ref.at[1], ref.at[0], right), ref.at[0]))
        mom_t.append((send(ref.at[1], ref.at[2], left), ref.at[2]))
    arrive(mt5, meta.at[:, :, 1 - c])

    info = jnp.zeros((8, BS), I32)
    for a in range(4):
        for b in range(4):
            for cc in range(2):
                info = info + meta[a, b, cc]
    info = info.astype(F32)
    sub = lax.broadcasted_iota(I32, (BS, BS), 0)
    lane = lax.broadcasted_iota(I32, (BS, BS), 1)
    subf = sub.astype(F32)
    lanef = lane.astype(F32)

    def upright(v):
        return jnp.sum(
            jnp.where(sub == lane, jnp.broadcast_to(v, (BS, BS)), 0.0), axis=1, keepdims=True
        )

    def total(v):
        return jnp.sum(v, axis=0, keepdims=True)

    def ones(mask):
        return jnp.where(mask, 1.0, 0.0)

    row, col, dst = info[0:1], info[1:2], info[2:3]
    row_t, col_t, dst_t = upright(row), upright(col), upright(dst)

    def order(major, minor, major_t, minor_t, span):
        key, key_t = major * span + minor, major_t * span + minor_t
        pos_t = jnp.sum(ones(key < key_t), axis=1, keepdims=True)
        hot = ones(pos_t == lanef)
        who = total(subf * hot)
        major_s = total(major_t * hot)
        minor_s = total(minor_t * hot)
        start = total(ones(major_t < major_s))
        keep = jnp.where(start == lanef[0:1], 0.0, 1.0)
        upto = total(ones(major_t <= lanef))
        has = upto - total(ones(major_t < lanef))
        return who, minor_s, keep, jnp.maximum(upto - 1.0, 0.0), jnp.minimum(has, 1.0)

    rows = list(order(col, row, col_t, row_t, 64.0))
    rows += list(order(row, col, row_t, col_t, 32.0))
    hot = ones(dst_t == lanef)
    rows += [total(subf * hot), total(row_t * hot), total(col_t * hot), total(hot)]
    top = [127, 63, 1, 127, 1, 127, 27, 1, 127, 1, 127, 63, 27, 1]
    for i, v in enumerate(rows):
        tab_v[i : i + 1, :] = jnp.clip(v.astype(I32), 0, top[i])
    tab_cp = local(tab_v, tab)

    z_event(2)
    for h in (0, 1):
        arrive(w2t[h, 0], w_all.at[w2(h, -1, c)])
        r = w_all.at[w2(h, -1, c) + (0,)]
        w2t[h, 2] = send(r, r, plus(1 - h))
        arrive(w2t[h, 1], w_all.at[w2(h, 1, c)])
        r = w_all.at[w2(h, 1, c) + (1,)]
        w2t[h, 3] = send(r, r, minus(1 - h))
        for i, delta in ((1, -1), (2, 1)):
            r = w_all.at[w2(h, delta, c)]
            wpt[h, i] = send(r, r, partner)
    z_event(3)
    z_event(4)
    for h in (0, 1):
        arrive(w2t[h, 2], w_all.at[w2(h, -2, c) + (0,)])
        arrive(w2t[h, 3], w_all.at[w2(h, 2, c) + (1,)])
        r = w_all.at[w2(h, 2, c)]
        wpt[h, 3] = send(r, r, partner)
    z_event(5)
    for h in (0, 1):
        for i, delta in ((0, 0), (1, -1), (2, 1), (3, 2)):
            arrive(wpt[h, i], w_all.at[w2(h, delta, 1 - c)])
    for cp in d_cp:
        cp.wait()
    tab_cp.wait()

    def wblock(s):
        return w_all[s // 32, lax.rem(s // 8, 4), lax.rem(s // 4, 2), lax.rem(s // 2, 2), lax.rem(s, 2)]

    def bwd(p, acc):
        prod = lax.dot_general(
            d_all[tab[6, p]], wblock(tab[5, p]), (((1,), (1,)), ((), ())),
            preferred_element_type=F32,
        )
        acc = acc * tab[7, p].astype(F32) + prod
        seg_b[p] = acc
        return acc

    lax.fori_loop(0, BS, bwd, jnp.zeros((BS, BS), F32), unroll=4)

    def own_part(r):
        return seg_b[tab[8, r]] * (tab[9, r].astype(F32) * SCALE)

    zr = {0: {}, 1: {}}

    def zr_send(dirn, i):
        k, h = (UP, DN)[dirn][i]
        level = m8(z + 5 - k) if dirn == 0 else m8(z - 5 + k)
        if i >= 2:
            arrive(zr[dirn][i - 2], zrecv.at[dirn, i - 2])

        def one(b, carry):
            v = own_part(level * 8 + h * 4 + b)
            if i >= 2:
                v = v + zrecv[dirn, i - 2, b].astype(F32)
            zsend[dirn, i, b] = v.astype(BF16)
            return carry

        lax.fori_loop(0, 4, one, 0, unroll=True)
        zr[dirn][i] = send(zsend.at[dirn, i], zrecv.at[dirn, i], zup if dirn == 0 else zdn)

    def zr_event(i):
        zr_send(0, i)
        zr_send(1, i)

    z_event_last = [zt[d][6] for d in (0, 1)]
    zr_event(0)
    zr_event(1)
    z_wait(0, 6)
    z_wait(1, 6)

    def grad(q):
        g = lax.dot_general(
            x_all[tab[11, q]], d_all[tab[12, q]], (((0,), (0,)), ((), ())),
            preferred_element_type=F32,
        )
        return g * (tab[13, q].astype(F32) * SCALE)

    gt = {}
    for a in range(4):
        def part(i, carry):
            b, k = i // 4, lax.rem(i, 4)
            q = ((a * 4 + b) * 2 + (1 - c)) * 4 + k
            g_out[a, b, k // 2, lax.rem(k, 2)] = grad(q).astype(BF16)
            return carry

        lax.fori_loop(0, 16, part, 0, unroll=4)
        gt[a] = send(g_out.at[a], g_in.at[a], partner)
        if a == 1:
            zr_event(2)
    for a in range(4):
        arrive(gt[a], g_in.at[a])

        def part(i, carry):
            b, k = i // 4, lax.rem(i, 4)
            q = ((a * 4 + b) * 2 + c) * 4 + k
            h, j = k // 2, lax.rem(k, 2)
            g_own[a, b, h, j] = (grad(q) + g_in[a, b, h, j].astype(F32)).astype(BF16)
            return carry

        lax.fori_loop(0, 16, part, 0, unroll=4)
        if a == 1:
            zr_event(3)

    def g1(h, delta, j):
        if h == 0:
            return (m4(x + delta), slice(None), 0, j)
        return (slice(None), m4(y + delta), 1, j)

    rt = {}
    for h in (0, 1):
        rt[h, 0, 0] = send(g_own.at[g1(h, 2, 0)], recv1.at[h, 0, 0], plus(h))
        rt[h, 1, 0] = send(g_own.at[g1(h, 2, 1)], recv1.at[h, 1, 0], minus(h))
    for h in (0, 1):
        rt[h, 0, 1] = send(g_own.at[g1(h, 1, 1)], recv1.at[h, 0, 1], plus(h))
        rt[h, 1, 1] = send(g_own.at[g1(h, -1, 0)], recv1.at[h, 1, 1], minus(h))

    def fwd(p, acc):
        prod = jnp.dot(x_all[tab[1, p]], wblock(tab[0, p]), preferred_element_type=F32)
        acc = acc * tab[2, p].astype(F32) + prod
        seg_f[p] = acc
        return acc

    acc = lax.fori_loop(0, 32, fwd, jnp.zeros((BS, BS), F32), unroll=4)
    zr_event(4)

    def g1_add(h, dirn):
        delta, j = (1, 0) if dirn == 0 else (-1, 1)
        arrive(rt[h, dirn, 0], recv1.at[h, dirn, 0])
        at = g1(h, delta, j)
        g_own[at] = (g_own[at].astype(F32) + recv1[h, dirn, 0].astype(F32)).astype(BF16)
        rt[h, dirn, 2] = send(
            g_own.at[at], recv1.at[h, dirn, 2], plus(h) if dirn == 0 else minus(h)
        )

    for h in (0, 1):
        g1_add(h, 0)
        g1_add(h, 1)
    acc = lax.fori_loop(32, 64, fwd, acc, unroll=4)
    zr_event(5)
    acc = lax.fori_loop(64, 96, fwd, acc, unroll=4)
    zr_event(6)

    for h in (0, 1):
        for dirn in (0, 1):
            arrive(rt[h, dirn, 1], recv1.at[h, dirn, 1])
            arrive(rt[h, dirn, 2], recv1.at[h, dirn, 2])
        for j in (0, 1):
            lo, hi = (2, 1) if j == 0 else (1, 2)
            q_sum[h, :, j] = (
                g_own[g1(h, 0, j)].astype(F32)
                + recv1[h, 0, lo].astype(F32)
                + recv1[h, 1, hi].astype(F32)
            ).astype(BF16)

    def pos2(h, delta):
        return m4(y + delta) if h == 0 else m4(x + delta)

    st = {}
    for h in (0, 1):
        st[h, 0, 0] = send(q_sum.at[h, pos2(h, 2), 0], recv2.at[h, 0, 0], plus(1 - h))
        st[h, 1, 0] = send(q_sum.at[h, pos2(h, 2), 1], recv2.at[h, 1, 0], minus(1 - h))
        st[h, 0, 1] = send(q_sum.at[h, pos2(h, 1), 1], recv2.at[h, 0, 1], plus(1 - h))
        st[h, 1, 1] = send(q_sum.at[h, pos2(h, -1), 0], recv2.at[h, 1, 1], minus(1 - h))
    acc = lax.fori_loop(96, 112, fwd, acc, unroll=4)
    for h in (0, 1):
        for dirn in (0, 1):
            delta, j = (1, 0) if dirn == 0 else (-1, 1)
            arrive(st[h, dirn, 0], recv2.at[h, dirn, 0])
            at = (h, pos2(h, delta), j)
            q_sum[at] = (q_sum[at].astype(F32) + recv2[h, dirn, 0].astype(F32)).astype(BF16)
            st[h, dirn, 2] = send(
                q_sum.at[at], recv2.at[h, dirn, 2], plus(1 - h) if dirn == 0 else minus(1 - h)
            )
    acc = lax.fori_loop(112, 128, fwd, acc, unroll=4)

    for i in range(28):
        v = seg_f[tab[3, i]] * (tab[4, i].astype(F32) * SCALE)
        hidden[:, i * BS : (i + 1) * BS] = v.astype(BF16)

    for dirn in (0, 1):
        arrive(zr[dirn][5], zrecv.at[dirn, 5])
        arrive(zr[dirn][6], zrecv.at[dirn, 6])
    for b in range(8):
        h, k = divmod(b, 4)
        v = own_part(z * 8 + b)
        v = v + zrecv[0, 5 if h == 1 else 6, k].astype(F32)
        v = v + zrecv[1, 5 if h == 0 else 6, k].astype(F32)
        in_grad[:, b * BS : (b + 1) * BS] = v.astype(BF16)

    for tag, region in mom_t:
        arrive(tag, region)
    for h in (0, 1):
        for dirn in (0, 1):
            arrive(st[h, dirn, 1], recv2.at[h, dirn, 1])
            arrive(st[h, dirn, 2], recv2.at[h, dirn, 2])
        for j in (0, 1):
            lo, hi = (2, 1) if j == 0 else (1, 2)
            g = (
                q_sum[h, pos2(h, 0), j].astype(F32)
                + recv2[h, 0, lo].astype(F32)
                + recv2[h, 1, hi].astype(F32)
            )
            q = dp * 4 + h * 2 + j
            s = tab[10, q]
            valid = tab[13, q].astype(F32)
            mi = jnp.clip(s - (dp - 1) * 4, 0, 11)
            first = B1 * mom1[mi // 4, lax.rem(mi, 4)] + (1.0 - B1) * g
            second = B2 * mom2[mi // 4, lax.rem(mi, 4)] + (1.0 - B2) * g * g
            stepped = wblock(s).astype(F32) - LEARN * first / (jnp.sqrt(second) + EPS)
            new_w[h * 2 + j] = (stepped * valid).astype(BF16)
            new_1[h * 2 + j] = first * valid
            new_2[h * 2 + j] = second * valid

    for cp in pending:
        cp.wait_send()


def body(weight, moment_one, moment_two, block_row, block_col, dest_slot, tokens, upstream):
    hbm = pl.BlockSpec(memory_space=pl.ANY)
    smem = pl.BlockSpec(memory_space=pltpu.SMEM)
    vmem = pl.BlockSpec(memory_space=pltpu.VMEM)
    return pl.pallas_call(
        kernel,
        name="step",
        out_shape=(
            jax.ShapeDtypeStruct((4, BS, BS), BF16),
            jax.ShapeDtypeStruct((4, BS, BS), F32),
            jax.ShapeDtypeStruct((4, BS, BS), F32),
            jax.ShapeDtypeStruct((128, 3584), BF16),
            jax.ShapeDtypeStruct((128, 1024), BF16),
        ),
        in_specs=[smem] * 3 + [hbm] * 5,
        out_specs=(vmem,) * 5,
        scratch_shapes=[
            pltpu.VMEM((64, BS, BS), BF16),
            pltpu.VMEM((4, 4, 2, 2, 2, BS, BS), BF16),
            pltpu.VMEM((4, 4, 2, 8, BS), I32),
            pltpu.VMEM((28, BS, BS), BF16),
            pltpu.VMEM((3, 4, BS, BS), F32),
            pltpu.VMEM((3, 4, BS, BS), F32),
            pltpu.VMEM((BS, BS, BS), F32),
            pltpu.VMEM((BS, BS, BS), F32),
            pltpu.VMEM((16, BS), I32),
            pltpu.SMEM((16, BS), I32),
            pltpu.VMEM((4, 4, 2, 2, BS, BS), BF16),
            pltpu.VMEM((4, 4, 2, 2, BS, BS), BF16),
            pltpu.VMEM((4, 4, 2, 2, BS, BS), BF16),
            pltpu.VMEM((2, 2, 3, 4, BS, BS), BF16),
            pltpu.VMEM((2, 4, 2, BS, BS), BF16),
            pltpu.VMEM((2, 2, 3, BS, BS), BF16),
            pltpu.VMEM((2, 7, 4, BS, BS), BF16),
            pltpu.VMEM((2, 7, 4, BS, BS), BF16),
            pltpu.SemaphoreType.DMA((48,)),
            pltpu.SemaphoreType.DMA((NSEM,)),
            pltpu.SemaphoreType.DMA((NSEM,)),
        ],
        compiler_params=pltpu.CompilerParams(
            collective_id=0, has_side_effects=True, vmem_limit_bytes=60 * 1024 * 1024
        ),
    )(block_row, block_col, dest_slot, weight, moment_one, moment_two, tokens, upstream)


def solution(mesh):
    return jax.shard_map(
        body,
        mesh=mesh,
        in_specs=(
            P(("dp", "mp"), None, None),
            P(("dp", "mp"), None, None),
            P(("dp", "mp"), None, None),
            P(("dp", "mp")),
            P(("dp", "mp")),
            P(("dp", "mp")),
            P("dp", "mp"),
            P("dp", "mp"),
        ),
        out_specs=(
            P(("dp", "mp"), None, None),
            P(("dp", "mp"), None, None),
            P(("dp", "mp"), None, None),
            P("dp", "mp"),
            P("dp", "mp"),
        ),
        check_vma=False,
    )
```

time: 267 us -> 87.5 us (0.33)
  waiting for transfers between devices: 118 us -> 0 us
  Pallas kernels: 0 us -> 79.1 us
  other arithmetic: 55.7 us -> 0 us
  matrix products: 27.8 us -> 0 us
  local copies, waits for them, and re-layouts: 28.9 us -> 6.78 us
  blocking collectives: 15.6 us -> 0 us
  between operations: 14.8 us -> 0.65 us
  starting transfers between devices: 4.88 us -> 0 us
    pallas_call x0 -> x1, Pallas kernels: none -> 79.1 us  [body(): pl.pallas_call(kernel, name='step', out_shape=(jax.ShapeDtypeStruct((4, B...]
    all_gather x2 -> x0, waiting for transfers between devices: 57.8 us -> none  [the longest x1 36.4 us: body(): lax.all_gather(weight, 'dp', axis=0, tiled=True)]
    reduce_scatter x2 -> x0, waiting for transfers between devices: 54.6 us -> none  [the longest x1 36.5 us: body(): lax.psum_scatter(partial_in, 'mp', scatter_dimension=1, tiled=True)]
    scatter-add x2 -> x0, other arithmetic: 44.2 us -> none  [the longest x1 27 us: body(): row_sums = jax.ops.segment_sum(backward, all_rows, num_segments=block_rows)]
    dot_general x7 -> x0, matrix products: 27.8 us -> none  [the longest x1 9.78 us: body(): jnp.einsum('tbj,bkj->btk', d_blocks, all_weight, preferred_element_type=j...]
    unnamed x1 -> x0, blocking collectives: 15.6 us -> none
    gather x2 -> x0, local copies, waits for them, and re-layouts: 6.08 us -> none  [the longest x1 3.06 us: body(): jnp.take(upstream.reshape(token_rows, block_cols, block_side), all_cols,...]
    mul x1 -> x0, local copies, waits for them, and re-layouts: 5.63 us -> none  [body(): jnp.swapaxes(row_sums, 0, 1) * grad_scale]
  transfers between devices with their start and end apart: 6 -> 0, of which waited for: 5 -> 0; matrix products, arithmetic and copies ran while one was open for 41% -> 0% of each run, Pallas kernels for 0% -> 0%
where the time goes in v1:
time: 87.5 us; the launch traced here: 86.5 us
  Pallas kernels  79.1 us (90%)
  local copies, waits for them, and re-layouts  6.78 us (8%)
    pallas_call x1, Pallas kernels, body(): pl.pallas_call(kernel, name='step', out_shape=(jax.ShapeDtypeStruct((4, B...  79.1 us
    unnamed x9, local copies, waits for them, and re-layouts  6.78 us

profile of v1, /device:TPU:2, one launch (start us, length us, event | category | flops | bytes accessed | tf_op | source)
XLA Modules:
  0.0 86.5 jit_solution(7967027986517930943)
XLA Ops:
  0.6 79.1 %step.1 = (bf16[4,128,128]{2,1,0:T(8,128)(2,1)}, f32[4,128,128]{2,1,0:T(8,128)}, f32[4,128,128]{2,1,0:T(8,128)}, bf16[128,3584]{1,0:T(8,128)(2,1)}, bf16[128,1024]{1,0:T(8,128)(2,1)}) custom-call(s32[4]{0:T(128)} %brow.1, s32[4]{0:T(128)} %bcol.1, s32[4]{0:T(128)} %bdst.1, bf16[4,128,128]{2,1,0:T(8,128)(2,1)} %weight.1, f32[4,128,128]{2,1,0:T(8,128)} %m1_in.1, ...), custom_call_target="tpu_custom_call" | custom-call | tf_op jit(solution)/shard_map/step/pallas_call | solution.py:475
  79.7 0.0 copy-start
  79.8 1.6 %copy.18 = bf16[4,128,128]{2,1,0:T(8,128)(2,1)} copy(bf16[4,128,128]{2,1,0:T(8,128)(2,1)} %get-tuple-element.10) | data formatting | bytes 262144
  81.4 1.7 %copy.19 = f32[4,128,128]{2,1,0:T(8,128)} copy(f32[4,128,128]{2,1,0:T(8,128)} %get-tuple-element.11) | data formatting | bytes 524288
  83.1 1.7 %copy.20 = f32[4,128,128]{2,1,0:T(8,128)} copy(f32[4,128,128]{2,1,0:T(8,128)} %get-tuple-element.12) | data formatting | bytes 524288
  84.7 0.0 copy-done
  84.7 0.0 copy-start.1
  84.7 0.9 %copy.21 = bf16[128,3584]{1,0:T(8,128)(2,1)} copy(bf16[128,3584]{1,0:T(8,128)(2,1)S(1)} %copy-done) | data formatting | bytes 1835008
  85.7 0.2 copy-done.1
  85.8 0.7 copy.22
Async XLA Ops:
  79.7 5.0 %copy-start = (bf16[128,3584]{1,0:T(8,128)(2,1)S(1)}, bf16[128,3584]{1,0:T(8,128)(2,1)}, u32[]{:S(2)}) copy-start(bf16[128,3584]{1,0:T(8,128)(2,1)} %get-tuple-element.13) | copy-start | bytes 2752516
  84.7 1.1 %copy-start.1 = (bf16[128,1024]{1,0:T(8,128)(2,1)S(1)}, bf16[128,1024]{1,0:T(8,128)(2,1)}, u32[]{:S(2)}) copy-start(bf16[128,1024]{1,0:T(8,128)(2,1)} %get-tuple-element.14) | copy-start | bytes 786436

commit v2 on v1

v2 whole, which is shorter than its diff:
```python
import math

import jax
import jax.numpy as jnp
from jax import lax
from jax.experimental import pallas as pl
from jax.experimental.pallas import tpu as pltpu
from jax.sharding import PartitionSpec as P

D = 8192
BS = 128
SCALE = 1.0 / math.sqrt(D)
LEARN = 0.02
B1 = 0.9
B2 = 0.95
EPS = 1e-08
NSEM = 256
MESH = pl.DeviceIdType.MESH

F32 = jnp.float32
BF16 = jnp.bfloat16
I32 = jnp.int32

UP = [(1, 0), (1, 1)] + [(k, s) for k in (2, 3, 4) for s in (2, 3, 0, 1)]
DN = [(1, 2), (1, 3)] + [(k, s) for k in (2, 3, 4) for s in (0, 1, 2, 3)]
OFF = (2, 1, -1, 0)


def kernel(
    brow, bcol, bdst, weight, m1_in, m2_in, tokens, upstream,
    new_w, new_1, new_2, hidden, in_grad,
    x_all, w_all, meta, d_all, mom1, mom2, seg_b, seg_f, tab_v, tab,
    g_out, g_in, g_own, recv1, q_sum, recv2, zsend, zrecv,
    lsem, ssem, rsem,
):
    dp = lax.axis_index("dp")
    z = lax.axis_index("mp")
    c = lax.rem(dp, 2)
    y = lax.rem(dp // 2, 4)
    x = dp // 8

    def dev(xx, yy, cc, zz):
        return {"dp": (xx * 4 + yy) * 2 + cc, "mp": zz}

    def m4(v):
        return lax.rem(v + 8, 4)

    def m8(v):
        return lax.rem(v + 16, 8)

    zup, zdn = dev(x, y, c, m8(z + 1)), dev(x, y, c, m8(z - 1))
    partner = dev(x, y, 1 - c, z)
    left = {"dp": lax.rem(dp + 31, 32), "mp": z}
    right = {"dp": lax.rem(dp + 1, 32), "mp": z}
    x2, y2 = dev(m4(x + 2), y, c, z), dev(x, m4(y + 2), c, z)
    xp, xm = dev(m4(x + 1), y, c, z), dev(m4(x - 1), y, c, z)
    yp, ym = dev(x, m4(y + 1), c, z), dev(x, m4(y - 1), c, z)

    def plus(h):
        return xp if h == 0 else yp

    def minus(h):
        return xm if h == 0 else ym

    counter = [0]
    pending = []

    def send(src, dst, device):
        i = counter[0]
        counter[0] += 1
        cp = pltpu.make_async_remote_copy(
            src_ref=src, dst_ref=dst, send_sem=ssem.at[i], recv_sem=rsem.at[i],
            device_id=device, device_id_type=MESH,
        )
        cp.start()
        pending.append(cp)
        return i, device

    def arrive(tag, region):
        i, device = tag
        pltpu.make_async_remote_copy(
            src_ref=region, dst_ref=region, send_sem=ssem.at[i], recv_sem=rsem.at[i],
            device_id=device, device_id_type=MESH,
        ).wait_recv()

    lcount = [0]

    def local(src, dst):
        i = lcount[0]
        lcount[0] += 1
        cp = pltpu.make_async_copy(src, dst, lsem.at[i])
        cp.start()
        return cp

    tok_cp = [local(tokens.at[:, pl.ds(i * BS, BS)], x_all.at[z * 8 + i]) for i in range(8)]
    w_cp = local(weight, w_all.at[pl.ds(dp * 4, 4)])
    d_cp = [local(upstream.at[:, pl.ds(i * BS, BS)], d_all.at[i]) for i in range(28)]
    mom_cp = [local(m1_in, mom1.at[1]), local(m2_in, mom2.at[1])]

    sub8 = lax.broadcasted_iota(I32, (8, BS), 0)
    lane8 = lax.broadcasted_iota(I32, (8, BS), 1)
    own_meta = jnp.zeros((8, BS), I32)
    for j in range(4):
        at = lane8 == dp * 4 + j
        for r, ref in enumerate((brow, bcol, bdst)):
            own_meta = own_meta + jnp.where(at & (sub8 == r), ref[j], 0)
    meta[x, y, c] = own_meta

    off = {"dp": lax.rem(dp + 31 + 2 * c, 32), "mp": z}
    barrier = pltpu.get_barrier_semaphore()
    for peer in (zup, zdn, partner, off, xp, xm, yp, ym, x2, y2):
        pl.semaphore_signal(barrier, inc=1, device_id=peer, device_id_type=MESH)
    pl.semaphore_wait(barrier, 10)

    zt = {0: {}, 1: {}}

    def xs(level, s):
        return x_all.at[pl.ds(level * 8 + s * 2, 2)]

    def z_part(dirn, i):
        k, s = divmod(i, 4)
        return k, s + 2 * dirn if k == 3 else s

    def z_send(dirn, i):
        k, s = z_part(dirn, i)
        r = xs(m8(z - k) if dirn == 0 else m8(z + k), s)
        zt[dirn][i] = send(r, r, zup if dirn == 0 else zdn)

    def z_wait(dirn, i):
        k, s = z_part(dirn, i)
        arrive(zt[dirn][i], xs(m8(z - k - 1) if dirn == 0 else m8(z + k + 1), s))

    def z_event(i):
        for dirn in (0, 1):
            z_wait(dirn, i)
            if i + 4 < 12:
                z_send(dirn, i + 4)
            elif i < 12 and (i - 8) // 2 == dirn:
                z_send(dirn, 12 + i % 2)

    def wp(h, du, dv, cc, j=None):
        xx, yy = (m4(x + du), m4(y + dv)) if h == 0 else (m4(x + dv), m4(y + du))
        base = ((xx * 4 + yy) * 2 + cc) * 4 + h * 2
        return w_all.at[pl.ds(base, 2)] if j is None else w_all.at[pl.ds(base + j, 1)]

    wt = {}

    def w_send(key, r, device):
        wt[key] = send(r, r, device)

    def w_partner(h, du, dv):
        w_send(("p", h, du, dv), wp(h, du, dv, c), partner)

    def w_phase2(h, du):
        r = wp(h, du, 0, c)
        w_send((2, h, du, 0), r, plus(1 - h))
        w_send((2, h, du, 1), r, minus(1 - h))
        w_partner(h, du, 0)

    def w_turn(h, du):
        arrive(wt[2, h, du, 0], wp(h, du, -1, c))
        w_send((3, h, du, 0), wp(h, du, -1, c, 0), plus(1 - h))
        arrive(wt[2, h, du, 1], wp(h, du, 1, c))
        w_send((3, h, du, 1), wp(h, du, 1, c, 1), minus(1 - h))
        w_partner(h, du, -1)
        w_partner(h, du, 1)

    def w_last(h, du):
        arrive(wt[3, h, du, 0], wp(h, du, -2, c, 0))
        arrive(wt[3, h, du, 1], wp(h, du, 2, c, 1))
        w_partner(h, du, 2)

    for i in range(4):
        tok_cp[2 * i].wait()
        tok_cp[2 * i + 1].wait()
        z_send(0, i)
        z_send(1, i)
    mt = [send(meta.at[x, y, c], meta.at[x, y, c], d) for d in (xp, xm, x2)]
    w_cp.wait()
    for h in (0, 1):
        w_send((0, h, 0), wp(h, 0, 0, c), plus(h))
        w_send((0, h, 1), wp(h, 0, 0, c), minus(h))
    for h in (0, 1):
        w_phase2(h, 0)

    for tag, delta in zip(mt, (-1, 1, 2)):
        arrive(tag, meta.at[m4(x + delta), y, c])
    mt = [send(meta.at[:, y, c], meta.at[:, y, c], d) for d in (yp, ym, y2)]
    for h in (0, 1):
        arrive(wt[0, h, 0], wp(h, -1, 0, c))
        w_send((1, h, 0), wp(h, -1, 0, c, 0), plus(h))
        arrive(wt[0, h, 1], wp(h, 1, 0, c))
        w_send((1, h, 1), wp(h, 1, 0, c, 1), minus(h))
    for h in (0, 1):
        w_phase2(h, -1)
        w_phase2(h, 1)
    z_event(0)
    z_event(1)
    for h in (0, 1):
        w_turn(h, 0)
    z_event(2)
    for tag, delta in zip(mt, (-1, 1, 2)):
        arrive(tag, meta.at[:, m4(y + delta), c])
    mt = send(meta.at[:, :, c], meta.at[:, :, c], partner)
    for h in (0, 1):
        arrive(wt[1, h, 0], wp(h, -2, 0, c, 0))
        arrive(wt[1, h, 1], wp(h, 2, 0, c, 1))
        w_phase2(h, 2)
    z_event(3)
    arrive(mt, meta.at[:, :, 1 - c])

    info = jnp.zeros((8, BS), I32)
    for a in range(4):
        for b in range(4):
            for cc in range(2):
                info = info + meta[a, b, cc]
    info = info.astype(F32)
    sub = lax.broadcasted_iota(I32, (BS, BS), 0)
    lane = lax.broadcasted_iota(I32, (BS, BS), 1)
    subf = sub.astype(F32)
    lanef = lane.astype(F32)

    def upright(v):
        return jnp.sum(
            jnp.where(sub == lane, jnp.broadcast_to(v, (BS, BS)), 0.0), axis=1, keepdims=True
        )

    def total(v):
        return jnp.sum(v, axis=0, keepdims=True)

    def ones(mask):
        return jnp.where(mask, 1.0, 0.0)

    row, col, dst = info[0:1], info[1:2], info[2:3]
    row_t, col_t, dst_t = upright(row), upright(col), upright(dst)

    def order(major, minor, major_t, minor_t, span):
        key, key_t = major * span + minor, major_t * span + minor_t
        pos_t = jnp.sum(ones(key < key_t), axis=1, keepdims=True)
        hot = ones(pos_t == lanef)
        who = total(subf * hot)
        major_s = total(major_t * hot)
        minor_s = total(minor_t * hot)
        start = total(ones(major_t < major_s))
        keep = jnp.where(start == lanef[0:1], 0.0, 1.0)
        upto = total(ones(major_t <= lanef))
        has = upto - total(ones(major_t < lanef))
        return who, minor_s, keep, jnp.maximum(upto - 1.0, 0.0), jnp.minimum(has, 1.0)

    z_event(4)
    rows = list(order(col, row, col_t, row_t, 64.0))
    rows += list(order(row, col, row_t, col_t, 32.0))
    hot = ones(dst_t == lanef)
    rows += [total(subf * hot), total(row_t * hot), total(col_t * hot), total(hot)]
    top = [127, 63, 1, 127, 1, 127, 27, 1, 127, 1, 127, 63, 27, 1]
    for i, v in enumerate(rows):
        tab_v[i : i + 1, :] = jnp.clip(v.astype(I32), 0, top[i])
    tab_cp = local(tab_v, tab)

    z_event(5)
    for h in (0, 1):
        w_turn(h, -1)
        w_turn(h, 1)
    z_event(6)
    for h in (0, 1):
        w_last(h, 0)
        w_turn(h, 2)
    z_event(7)
    for h in (0, 1):
        w_last(h, -1)
        w_last(h, 1)
    z_event(8)
    for h in (0, 1):
        w_last(h, 2)
    z_event(9)

    for cp in mom_cp:
        cp.wait()
    mom_t = []
    for ref in (mom1, mom2):
        mom_t.append((send(ref.at[1], ref.at[0], right), ref.at[0]))
        mom_t.append((send(ref.at[1], ref.at[2], left), ref.at[2]))

    for h in (0, 1):
        for du in OFF:
            for dv in OFF:
                arrive(wt["p", h, du, dv], wp(h, du, dv, 1 - c))
    for cp in d_cp:
        cp.wait()
    tab_cp.wait()

    def run(start, stop, step, acc):
        def some(t, acc):
            for i in range(16):
                acc = step(start + t * 16 + i, acc)
            return acc

        return lax.fori_loop(0, (stop - start) // 16, some, acc)

    def bwd(p, acc):
        prod = lax.dot_general(
            d_all[tab[6, p]], w_all[tab[5, p]], (((1,), (1,)), ((), ())),
            preferred_element_type=F32,
        )
        acc = acc * tab[7, p].astype(F32) + prod
        seg_b[p] = acc
        return acc

    acc = run(0, 48, bwd, jnp.zeros((BS, BS), F32))
    z_event(10)
    acc = run(48, 96, bwd, acc)
    z_event(11)
    acc = run(96, 128, bwd, acc)

    def own_part(r):
        return seg_b[tab[8, r]] * (tab[9, r].astype(F32) * SCALE)

    zr = {0: {}, 1: {}}

    def zr_send(dirn, i):
        k, s = (UP, DN)[dirn][i]
        level = m8(z + 5 - k) if dirn == 0 else m8(z - 5 + k)
        if i >= 4:
            arrive(zr[dirn][i - 4], zrecv.at[dirn, i - 4])
        for b in range(2):
            v = own_part(level * 8 + s * 2 + b)
            if i >= 4:
                v = v + zrecv[dirn, i - 4, b].astype(F32)
            zsend[dirn, i, b] = v.astype(BF16)
        zr[dirn][i] = send(zsend.at[dirn, i], zrecv.at[dirn, i], zup if dirn == 0 else zdn)

    def zr_event(i):
        zr_send(0, i)
        zr_send(1, i)

    for i in range(4):
        zr_event(i)
    z_event(12)
    z_event(13)

    def grad(g, h, j, o, cc):
        u, v = OFF[g], OFF[o]
        xx, yy = (m4(x + u), m4(y + v)) if h == 0 else (m4(x + v), m4(y + u))
        q = ((xx * 4 + yy) * 2 + cc) * 4 + h * 2 + j
        r = lax.dot_general(
            x_all[tab[11, q]], d_all[tab[12, q]], (((0,), (0,)), ((), ())),
            preferred_element_type=F32,
        )
        return r * (tab[13, q].astype(F32) * SCALE)

    gt = {}
    members = [(h, j, o) for h in (0, 1) for j in (0, 1) for o in range(4)]
    for g in range(4):
        for h, j, o in members:
            g_out[g, h, j, o] = grad(g, h, j, o, 1 - c).astype(BF16)
        gt[g] = send(g_out.at[g], g_in.at[g], partner)

    def fwd(p, acc):
        prod = jnp.dot(x_all[tab[1, p]], w_all[tab[0, p]], preferred_element_type=F32)
        acc = acc * tab[2, p].astype(F32) + prod
        seg_f[p] = acc
        return acc

    facc = run(0, 32, fwd, jnp.zeros((BS, BS), F32))

    rt = {}

    def g1_send(key, src, device):
        h, dirn, n = key
        rt[key] = send(src, recv1.at[h, dirn, n], device)

    for g in range(4):
        arrive(gt[g], g_in.at[g])
        for h, j, o in members:
            v = grad(g, h, j, o, c) + g_in[g, h, j, o].astype(F32)
            g_own[g, h, j, o] = v.astype(BF16)
        for h in (0, 1):
            if g == 0:
                g1_send((h, 0, 0), g_own.at[0, h, 0], plus(h))
                g1_send((h, 1, 0), g_own.at[0, h, 1], minus(h))
            elif g == 1:
                g1_send((h, 0, 1), g_own.at[1, h, 1], plus(h))
            elif g == 2:
                g1_send((h, 1, 1), g_own.at[2, h, 0], minus(h))
        if g == 1:
            zr_event(4)
    zr_event(5)
    facc = run(32, 64, fwd, facc)
    zr_event(6)
    facc = run(64, 80, fwd, facc)
    zr_event(7)
    for h in (0, 1):
        for dirn in (0, 1):
            arrive(rt[h, dirn, 0], recv1.at[h, dirn, 0])
            at = (1, h, 0) if dirn == 0 else (2, h, 1)
            g_own[at] = (g_own[at].astype(F32) + recv1[h, dirn, 0].astype(F32)).astype(BF16)
            g1_send((h, dirn, 2), g_own.at[at], plus(h) if dirn == 0 else minus(h))
    zr_event(8)
    facc = run(80, 96, fwd, facc)
    zr_event(9)
    facc = run(96, 128, fwd, facc)
    zr_event(10)
    for i in range(28):
        v = seg_f[tab[3, i]] * (tab[4, i].astype(F32) * SCALE)
        hidden[:, i * BS : (i + 1) * BS] = v.astype(BF16)
    zr_event(11)

    st = {}

    def g2_send(key, src, device):
        h, dirn, n = key
        st[key] = send(src, recv2.at[h, dirn, n], device)

    for h in (0, 1):
        for dirn in (0, 1):
            arrive(rt[h, dirn, 1], recv1.at[h, dirn, 1])
            arrive(rt[h, dirn, 2], recv1.at[h, dirn, 2])
        for j in (0, 1):
            lo, hi = (2, 1) if j == 0 else (1, 2)
            q_sum[h, j] = (
                g_own[3, h, j].astype(F32)
                + recv1[h, 0, lo].astype(F32)
                + recv1[h, 1, hi].astype(F32)
            ).astype(BF16)
        g2_send((h, 0, 0), q_sum.at[h, 0, 0], plus(1 - h))
        g2_send((h, 1, 0), q_sum.at[h, 1, 0], minus(1 - h))
        g2_send((h, 0, 1), q_sum.at[h, 1, 1], plus(1 - h))
        g2_send((h, 1, 1), q_sum.at[h, 0, 2], minus(1 - h))
    zr_event(12)
    zr_event(13)
    for h in (0, 1):
        for dirn in (0, 1):
            arrive(st[h, dirn, 0], recv2.at[h, dirn, 0])
            at = (h, 0, 1) if dirn == 0 else (h, 1, 2)
            q_sum[at] = (q_sum[at].astype(F32) + recv2[h, dirn, 0].astype(F32)).astype(BF16)
            g2_send((h, dirn, 2), q_sum.at[at], plus(1 - h) if dirn == 0 else minus(1 - h))

    for s in (2, 3, 0, 1):
        iu, id_ = UP.index((4, s)), DN.index((4, s))
        arrive(zr[0][iu], zrecv.at[0, iu])
        arrive(zr[1][id_], zrecv.at[1, id_])
        for k in range(2):
            b = s * 2 + k
            v = own_part(z * 8 + b) + zrecv[0, iu, k].astype(F32) + zrecv[1, id_, k].astype(F32)
            in_grad[:, b * BS : (b + 1) * BS] = v.astype(BF16)

    for tag, region in mom_t:
        arrive(tag, region)
    for h in (0, 1):
        for dirn in (0, 1):
            arrive(st[h, dirn, 1], recv2.at[h, dirn, 1])
            arrive(st[h, dirn, 2], recv2.at[h, dirn, 2])
        for j in (0, 1):
            lo, hi = (2, 1) if j == 0 else (1, 2)
            g = (
                q_sum[h, j, 3].astype(F32)
                + recv2[h, 0, lo].astype(F32)
                + recv2[h, 1, hi].astype(F32)
            )
            q = dp * 4 + h * 2 + j
            s = tab[10, q]
            valid = tab[13, q].astype(F32)
            mi = jnp.clip(s - (dp - 1) * 4, 0, 11)
            first = B1 * mom1[mi // 4, lax.rem(mi, 4)] + (1.0 - B1) * g
            second = B2 * mom2[mi // 4, lax.rem(mi, 4)] + (1.0 - B2) * g * g
            stepped = w_all[s].astype(F32) - LEARN * first / (jnp.sqrt(second) + EPS)
            new_w[h * 2 + j] = (stepped * valid).astype(BF16)
            new_1[h * 2 + j] = first * valid
            new_2[h * 2 + j] = second * valid

    for cp in pending:
        cp.wait_send()


def store(a, b, c, d, e, oa, ob, oc, od, oe, sem):
    copies = [
        pltpu.make_async_copy(src, dst, sem.at[i])
        for i, (src, dst) in enumerate(((a, oa), (b, ob), (c, oc), (d, od), (e, oe)))
    ]
    for cp in copies:
        cp.start()
    for cp in copies:
        cp.wait()


def body(weight, moment_one, moment_two, block_row, block_col, dest_slot, tokens, upstream):
    hbm = pl.BlockSpec(memory_space=pl.ANY)
    smem = pl.BlockSpec(memory_space=pltpu.SMEM)
    vmem = pl.BlockSpec(memory_space=pltpu.VMEM)
    outs = (
        ((4, BS, BS), BF16), ((4, BS, BS), F32), ((4, BS, BS), F32),
        ((128, 3584), BF16), ((128, 1024), BF16),
    )
    made = pl.pallas_call(
        kernel,
        name="step",
        out_shape=tuple(pltpu.VMEM(s, t) for s, t in outs),
        in_specs=[smem] * 3 + [hbm] * 5,
        out_specs=(vmem,) * 5,
        scratch_shapes=[
            pltpu.VMEM((64, BS, BS), BF16),
            pltpu.VMEM((BS, BS, BS), BF16),
            pltpu.VMEM((4, 4, 2, 8, BS), I32),
            pltpu.VMEM((28, BS, BS), BF16),
            pltpu.VMEM((3, 4, BS, BS), F32),
            pltpu.VMEM((3, 4, BS, BS), F32),
            pltpu.VMEM((BS, BS, BS), F32),
            pltpu.VMEM((BS, BS, BS), F32),
            pltpu.VMEM((16, BS), I32),
            pltpu.SMEM((16, BS), I32),
            pltpu.VMEM((4, 2, 2, 4, BS, BS), BF16),
            pltpu.VMEM((4, 2, 2, 4, BS, BS), BF16),
            pltpu.VMEM((4, 2, 2, 4, BS, BS), BF16),
            pltpu.VMEM((2, 2, 3, 4, BS, BS), BF16),
            pltpu.VMEM((2, 2, 4, BS, BS), BF16),
            pltpu.VMEM((2, 2, 3, BS, BS), BF16),
            pltpu.VMEM((2, 14, 2, BS, BS), BF16),
            pltpu.VMEM((2, 14, 2, BS, BS), BF16),
            pltpu.SemaphoreType.DMA((48,)),
            pltpu.SemaphoreType.DMA((NSEM,)),
            pltpu.SemaphoreType.DMA((NSEM,)),
        ],
        compiler_params=pltpu.CompilerParams(
            collective_id=0, has_side_effects=True, vmem_limit_bytes=62 * 1024 * 1024
        ),
    )(block_row, block_col, dest_slot, weight, moment_one, moment_two, tokens, upstream)
    return pl.pallas_call(
        store,
        name="store",
        out_shape=tuple(jax.ShapeDtypeStruct(s, t) for s, t in outs),
        in_specs=[pl.BlockSpec(memory_space=pltpu.VMEM)] * 5,
        out_specs=(hbm,) * 5,
        scratch_shapes=[pltpu.SemaphoreType.DMA((5,))],
        compiler_params=pltpu.CompilerParams(vmem_limit_bytes=2 * 1024 * 1024),
    )(*made)


def solution(mesh):
    return jax.shard_map(
        body,
        mesh=mesh,
        in_specs=(
            P(("dp", "mp"), None, None),
            P(("dp", "mp"), None, None),
            P(("dp", "mp"), None, None),
            P(("dp", "mp")),
            P(("dp", "mp")),
            P(("dp", "mp")),
            P("dp", "mp"),
            P("dp", "mp"),
        ),
        out_specs=(
            P(("dp", "mp"), None, None),
            P(("dp", "mp"), None, None),
            P(("dp", "mp"), None, None),
            P("dp", "mp"),
            P("dp", "mp"),
        ),
        check_vma=False,
    )
```

time: 87.5 us -> 61.7 us (0.71)
  Pallas kernels: 79.1 us -> 59.9 us
  local copies, waits for them, and re-layouts: 6.78 us -> 0 us
    pallas_call x1 -> x2, Pallas kernels: 79.1 us -> 59.9 us  [the longest x1 58.6 us: body(): pl.pallas_call(kernel, name='step', out_shape=tuple((pltpu.VMEM(s, t) for...]
    unnamed x9 -> x0, local copies, waits for them, and re-layouts: 6.78 us -> none
where the time goes in v2:
time: 61.7 us; the launch traced here: 60.5 us
  Pallas kernels  59.9 us (97%)
  between operations  0.64 us (1%)
    pallas_call x1, Pallas kernels, body(): pl.pallas_call(kernel, name='step', out_shape=tuple((pltpu.VMEM(s, t) for...  58.6 us
    pallas_call x1, Pallas kernels, body(): pl.pallas_call(store, name='store', out_shape=tuple((jax.ShapeDtypeStruct...  1.27 us

profile of v2, /device:TPU:2, one launch (start us, length us, event | category | flops | bytes accessed | tf_op | source)
XLA Modules:
  0.0 60.5 jit_solution(7724745155404107265)
XLA Ops:
  0.6 58.6 %step.1 = (bf16[4,128,128]{2,1,0:T(8,128)(2,1)S(1)}, f32[4,128,128]{2,1,0:T(8,128)S(1)}, f32[4,128,128]{2,1,0:T(8,128)S(1)}, bf16[128,3584]{1,0:T(8,128)(2,1)S(1)}, bf16[128,1024]{1,0:T(8,128)(2,1)S(1)}) custom-call(s32[4]{0:T(128)} %brow.1, s32[4]{0:T(128)} %bcol.1, s32[4]{0:T(128)} %bdst.1, bf16[4,128,128]{2,1,0:T(8,128)(2,1)} %weight.1, ...), custom_call_target="tpu_custom_call" | custom-call | tf_op jit(solution)/shard_map/step/pallas_call | solution.py:494
  59.3 1.3 %store.1 = (bf16[4,128,128]{2,1,0:T(8,128)(2,1)}, f32[4,128,128]{2,1,0:T(8,128)}, f32[4,128,128]{2,1,0:T(8,128)}, bf16[128,3584]{1,0:T(8,128)(2,1)}, bf16[128,1024]{1,0:T(8,128)(2,1)}) custom-call(bf16[4,128,128]{2,1,0:T(8,128)(2,1)S(1)} %get-tuple-element.10.a, f32[4,128,128]{2,1,0:T(8,128)S(1)} %get-tuple-element.11.b, ...), custom_call_target="tpu_custom_call" | custom-call | tf_op jit(solution)/shard_map/store/pallas_call | solution.py:527

commit v3 on v2

--- a/solution.py
+++ b/solution.py
@@ -29,7 +29,7 @@
 def kernel(
     brow, bcol, bdst, weight, m1_in, m2_in, tokens, upstream,
     new_w, new_1, new_2, hidden, in_grad,
-    x_all, w_all, meta, d_all, mom1, mom2, seg_b, seg_f, tab_v, tab,
+    x_all, w_all, w_far, meta, d_all, d_turn, mom1, mom2, seg_b, seg_f, tab_v, tab,
     g_out, g_in, g_own, recv1, q_sum, recv2, zsend, zrecv,
     lsem, ssem, rsem,
 ):
@@ -92,6 +92,11 @@
         cp.start()
         return cp
 
+    off = {"dp": lax.rem(dp + 31 + 2 * c, 32), "mp": z}
+    barrier = pltpu.get_barrier_semaphore()
+    for peer in (zup, zdn, partner, off, xp, xm, yp, ym, x2, y2):
+        pl.semaphore_signal(barrier, inc=1, device_id=peer, device_id_type=MESH)
+
     tok_cp = [local(tokens.at[:, pl.ds(i * BS, BS)], x_all.at[z * 8 + i]) for i in range(8)]
     w_cp = local(weight, w_all.at[pl.ds(dp * 4, 4)])
     d_cp = [local(upstream.at[:, pl.ds(i * BS, BS)], d_all.at[i]) for i in range(28)]
@@ -106,10 +111,6 @@
             own_meta = own_meta + jnp.where(at & (sub8 == r), ref[j], 0)
     meta[x, y, c] = own_meta
 
-    off = {"dp": lax.rem(dp + 31 + 2 * c, 32), "mp": z}
-    barrier = pltpu.get_barrier_semaphore()
-    for peer in (zup, zdn, partner, off, xp, xm, yp, ym, x2, y2):
-        pl.semaphore_signal(barrier, inc=1, device_id=peer, device_id_type=MESH)
     pl.semaphore_wait(barrier, 10)
 
     zt = {0: {}, 1: {}}
@@ -118,8 +119,7 @@
         return x_all.at[pl.ds(level * 8 + s * 2, 2)]
 
     def z_part(dirn, i):
-        k, s = divmod(i, 4)
-        return k, s + 2 * dirn if k == 3 else s
+        return i // 4, (i + 2 * dirn) % 4
 
     def z_send(dirn, i):
         k, s = z_part(dirn, i)
@@ -133,15 +133,17 @@
     def z_event(i):
         for dirn in (0, 1):
             z_wait(dirn, i)
-            if i + 4 < 12:
+            if i + 4 < 14:
                 z_send(dirn, i + 4)
-            elif i < 12 and (i - 8) // 2 == dirn:
-                z_send(dirn, 12 + i % 2)
 
     def wp(h, du, dv, cc, j=None):
         xx, yy = (m4(x + du), m4(y + dv)) if h == 0 else (m4(x + dv), m4(y + du))
         base = ((xx * 4 + yy) * 2 + cc) * 4 + h * 2
         return w_all.at[pl.ds(base, 2)] if j is None else w_all.at[pl.ds(base + j, 1)]
+
+    def wf(h, du, cc, j=None):
+        base = ((h * 4 + (m4(x + du) if h == 0 else m4(y + du))) * 2 + cc) * 2
+        return w_far.at[pl.ds(base, 2)] if j is None else w_far.at[pl.ds(base + j, 1)]
 
     wt = {}
 
@@ -159,20 +161,20 @@
 
     def w_turn(h, du):
         arrive(wt[2, h, du, 0], wp(h, du, -1, c))
-        w_send((3, h, du, 0), wp(h, du, -1, c, 0), plus(1 - h))
+        wt[3, h, du, 0] = send(wp(h, du, -1, c, 0), wf(h, du, c, 0), plus(1 - h))
         arrive(wt[2, h, du, 1], wp(h, du, 1, c))
-        w_send((3, h, du, 1), wp(h, du, 1, c, 1), minus(1 - h))
+        wt[3, h, du, 1] = send(wp(h, du, 1, c, 1), wf(h, du, c, 1), minus(1 - h))
         w_partner(h, du, -1)
         w_partner(h, du, 1)
 
     def w_last(h, du):
-        arrive(wt[3, h, du, 0], wp(h, du, -2, c, 0))
-        arrive(wt[3, h, du, 1], wp(h, du, 2, c, 1))
-        w_partner(h, du, 2)
-
+        arrive(wt[3, h, du, 0], wf(h, du, c, 0))
+        arrive(wt[3, h, du, 1], wf(h, du, c, 1))
+        w_send(("p", h, du, 2), wf(h, du, c), partner)
+
+    for cp in tok_cp:
+        cp.wait()
     for i in range(4):
-        tok_cp[2 * i].wait()
-        tok_cp[2 * i + 1].wait()
         z_send(0, i)
         z_send(1, i)
     mt = [send(meta.at[x, y, c], meta.at[x, y, c], d) for d in (xp, xm, x2)]
@@ -183,9 +185,15 @@
     for h in (0, 1):
         w_phase2(h, 0)
 
+    for cp in d_cp:
+        cp.wait()
+    for i in range(28):
+        d_turn[i] = d_all[i].T
+
     for tag, delta in zip(mt, (-1, 1, 2)):
         arrive(tag, meta.at[m4(x + delta), y, c])
     mt = [send(meta.at[:, y, c], meta.at[:, y, c], d) for d in (yp, ym, y2)]
+    z_event(0)
     for h in (0, 1):
         arrive(wt[0, h, 0], wp(h, -1, 0, c))
         w_send((1, h, 0), wp(h, -1, 0, c, 0), plus(h))
@@ -194,11 +202,11 @@
     for h in (0, 1):
         w_phase2(h, -1)
         w_phase2(h, 1)
-    z_event(0)
     z_event(1)
+    z_event(2)
     for h in (0, 1):
         w_turn(h, 0)
-    z_event(2)
+    z_event(3)
     for tag, delta in zip(mt, (-1, 1, 2)):
         arrive(tag, meta.at[:, m4(y + delta), c])
     mt = send(meta.at[:, :, c], meta.at[:, :, c], partner)
@@ -206,7 +214,7 @@
         arrive(wt[1, h, 0], wp(h, -2, 0, c, 0))
         arrive(wt[1, h, 1], wp(h, 2, 0, c, 1))
         w_phase2(h, 2)
-    z_event(3)
+    z_event(4)
     arrive(mt, meta.at[:, :, 1 - c])
 
     info = jnp.zeros((8, BS), I32)
@@ -234,11 +242,11 @@
     row, col, dst = info[0:1], info[1:2], info[2:3]
     row_t, col_t, dst_t = upright(row), upright(col), upright(dst)
 
-    def order(major, minor, major_t, minor_t, span):
+    def order(major, minor, major_t, minor_t, span, name_t):
         key, key_t = major * span + minor, major_t * span + minor_t
         pos_t = jnp.sum(ones(key < key_t), axis=1, keepdims=True)
         hot = ones(pos_t == lanef)
-        who = total(subf * hot)
+        who = total(name_t * hot)
         major_s = total(major_t * hot)
         minor_s = total(minor_t * hot)
         start = total(ones(major_t < major_s))
@@ -247,9 +255,23 @@
         has = upto - total(ones(major_t < lanef))
         return who, minor_s, keep, jnp.maximum(upto - 1.0, 0.0), jnp.minimum(has, 1.0)
 
-    z_event(4)
-    rows = list(order(col, row, col_t, row_t, 64.0))
-    rows += list(order(row, col, row_t, col_t, 32.0))
+    lane1 = lane8[0:1]
+    first_half = lax.rem(lane1 // 2, 2) == 0
+    far = jnp.where(
+        first_half, ones(lax.rem(lane1 // 8, 4) == m4(y + 2)), ones(lane1 // 32 == m4(x + 2))
+    )
+    major = far * 64.0 + row
+    lane_row = jnp.where(first_half, lane1 // 32, 4 + lax.rem(lane1 // 8, 4))
+    in_far = lane_row * 4 + lax.rem(lane1 // 4, 2) * 2 + lax.rem(lane1, 2)
+    name = jnp.where(far > 0.0, in_far, lane1).astype(F32)
+    rows = list(order(major, col, upright(major), col_t, 32.0, upright(name)))
+    rows[0] = jnp.where(lane1 < 96, rows[0], jnp.minimum(rows[0], 31.0))
+    z_event(5)
+    for h in (0, 1):
+        w_turn(h, -1)
+        w_turn(h, 1)
+    rows = list(order(col, row, col_t, row_t, 64.0, subf)) + rows
+    z_event(6)
     hot = ones(dst_t == lanef)
     rows += [total(subf * hot), total(row_t * hot), total(col_t * hot), total(hot)]
     top = [127, 63, 1, 127, 1, 127, 27, 1, 127, 1, 127, 63, 27, 1]
@@ -257,36 +279,22 @@
         tab_v[i : i + 1, :] = jnp.clip(v.astype(I32), 0, top[i])
     tab_cp = local(tab_v, tab)
 
-    z_event(5)
-    for h in (0, 1):
-        w_turn(h, -1)
-        w_turn(h, 1)
-    z_event(6)
     for h in (0, 1):
         w_last(h, 0)
+    z_event(7)
+    for h in (0, 1):
         w_turn(h, 2)
-    z_event(7)
+    z_event(8)
     for h in (0, 1):
         w_last(h, -1)
         w_last(h, 1)
-    z_event(8)
+    z_event(9)
     for h in (0, 1):
         w_last(h, 2)
-    z_event(9)
-
-    for cp in mom_cp:
-        cp.wait()
-    mom_t = []
-    for ref in (mom1, mom2):
-        mom_t.append((send(ref.at[1], ref.at[0], right), ref.at[0]))
-        mom_t.append((send(ref.at[1], ref.at[2], left), ref.at[2]))
-
     for h in (0, 1):
         for du in OFF:
-            for dv in OFF:
+            for dv in (0, -1, 1):
                 arrive(wt["p", h, du, dv], wp(h, du, dv, 1 - c))
-    for cp in d_cp:
-        cp.wait()
     tab_cp.wait()
 
     def run(start, stop, step, acc):
@@ -297,23 +305,24 @@
 
         return lax.fori_loop(0, (stop - start) // 16, some, acc)
 
-    def bwd(p, acc):
+    def bwd(p, acc, blocks=w_all, top=127):
         prod = lax.dot_general(
-            d_all[tab[6, p]], w_all[tab[5, p]], (((1,), (1,)), ((), ())),
+            blocks[jnp.minimum(tab[5, p], top)], d_turn[tab[6, p]], (((1,), (0,)), ((), ())),
             preferred_element_type=F32,
         )
         acc = acc * tab[7, p].astype(F32) + prod
         seg_b[p] = acc
         return acc
 
-    acc = run(0, 48, bwd, jnp.zeros((BS, BS), F32))
-    z_event(10)
-    acc = run(48, 96, bwd, acc)
-    z_event(11)
-    acc = run(96, 128, bwd, acc)
+    acc = run(0, 96, bwd, jnp.zeros((BS, BS), F32))
+    for h in (0, 1):
+        for du in OFF:
+            arrive(wt["p", h, du, 2], wf(h, du, 1 - c))
+    acc = run(96, 128, lambda p, acc: bwd(p, acc, w_far, 31), acc)
 
     def own_part(r):
-        return seg_b[tab[8, r]] * (tab[9, r].astype(F32) * SCALE)
+        near = seg_b[tab[8, r]] * (tab[9, r].astype(F32) * SCALE)
+        return near + seg_b[tab[8, 64 + r]] * (tab[9, 64 + r].astype(F32) * SCALE)
 
     zr = {0: {}, 1: {}}
 
@@ -335,8 +344,15 @@
 
     for i in range(4):
         zr_event(i)
-    z_event(12)
-    z_event(13)
+
+    for cp in mom_cp:
+        cp.wait()
+    mom_t = []
+    for ref in (mom1, mom2):
+        mom_t.append((send(ref.at[1], ref.at[0], right), ref.at[0]))
+        mom_t.append((send(ref.at[1], ref.at[2], left), ref.at[2]))
+    for i in range(10, 14):
+        z_event(i)
 
     def grad(g, h, j, o, cc):
         u, v = OFF[g], OFF[o]
@@ -349,11 +365,12 @@
         return r * (tab[13, q].astype(F32) * SCALE)
 
     gt = {}
-    members = [(h, j, o) for h in (0, 1) for j in (0, 1) for o in range(4)]
+    members = [(j, o) for j in (0, 1) for o in range(4)]
     for g in range(4):
-        for h, j, o in members:
-            g_out[g, h, j, o] = grad(g, h, j, o, 1 - c).astype(BF16)
-        gt[g] = send(g_out.at[g], g_in.at[g], partner)
+        for h in (0, 1):
+            for j, o in members:
+                g_out[g, h, j, o] = grad(g, h, j, o, 1 - c).astype(BF16)
+            gt[g, h] = send(g_out.at[g, h], g_in.at[g, h], partner)
 
     def fwd(p, acc):
         prod = jnp.dot(x_all[tab[1, p]], w_all[tab[0, p]], preferred_element_type=F32)
@@ -361,91 +378,146 @@
         seg_f[p] = acc
         return acc
 
+    zr_event(4)
+    for h in (0, 1):
+        for a in range(4):
+            xx, yy = (a, m4(y + 2)) if h == 0 else (m4(x + 2), a)
+            for cc in (0, 1):
+                for j in (0, 1):
+                    w_all[((xx * 4 + yy) * 2 + cc) * 4 + h * 2 + j] = w_far[((h * 4 + a) * 2 + cc) * 2 + j]
     facc = run(0, 32, fwd, jnp.zeros((BS, BS), F32))
 
     rt = {}
 
-    def g1_send(key, src, device):
-        h, dirn, n = key
-        rt[key] = send(src, recv1.at[h, dirn, n], device)
-
-    for g in range(4):
-        arrive(gt[g], g_in.at[g])
-        for h, j, o in members:
-            v = grad(g, h, j, o, c) + g_in[g, h, j, o].astype(F32)
-            g_own[g, h, j, o] = v.astype(BF16)
+    def halves(ref, u):
+        return ref.at[pl.ds(2 * u, 2)]
+
+    def g1_send(h, dirn, n, u, g, j):
+        rt[h, dirn, n, u] = send(
+            g_own.at[g, h, j, pl.ds(2 * u, 2)], recv1.at[h, dirn, n, pl.ds(2 * u, 2)],
+            plus(h) if dirn == 0 else minus(h),
+        )
+
+    def g1_direct(h, dirn, u):
+        g1_send(h, dirn, 1, u, 1 + dirn, 1 - dirn)
+
+    def g1_arrive(h, dirn, n, u):
+        arrive(rt[h, dirn, n, u], recv1.at[h, dirn, n, pl.ds(2 * u, 2)])
+
+    def own_group(g):
         for h in (0, 1):
+            arrive(gt[g, h], g_in.at[g, h])
+            for j, o in members:
+                v = grad(g, h, j, o, c) + g_in[g, h, j, o].astype(F32)
+                g_own[g, h, j, o] = v.astype(BF16)
             if g == 0:
-                g1_send((h, 0, 0), g_own.at[0, h, 0], plus(h))
-                g1_send((h, 1, 0), g_own.at[0, h, 1], minus(h))
-            elif g == 1:
-                g1_send((h, 0, 1), g_own.at[1, h, 1], plus(h))
-            elif g == 2:
-                g1_send((h, 1, 1), g_own.at[2, h, 0], minus(h))
-        if g == 1:
-            zr_event(4)
+                for u in (0, 1):
+                    g1_send(h, 0, 0, u, 0, 0)
+                    g1_send(h, 1, 0, u, 0, 1)
+            elif g < 3:
+                g1_direct(h, g - 1, 0)
+
+    def g1_step(u):
+        for h in (0, 1):
+            for dirn in (0, 1):
+                g1_arrive(h, dirn, 0, u)
+                g, j = (1, 0) if dirn == 0 else (2, 1)
+                for o in (2 * u, 2 * u + 1):
+                    v = g_own[g, h, j, o].astype(F32) + recv1[h, dirn, 0, o].astype(F32)
+                    g_own[g, h, j, o] = v.astype(BF16)
+                g1_send(h, dirn, 2, u, g, j)
+                if u == 0:
+                    g1_direct(h, dirn, 1)
+
+    st = {}
+
+    def g2_send(h, dirn, n, j, o):
+        st[h, dirn, n] = send(
+            q_sum.at[h, j, o], recv2.at[h, dirn, n], plus(1 - h) if dirn == 0 else minus(1 - h)
+        )
+
+    def g1_end(u):
+        for h in (0, 1):
+            for dirn in (0, 1):
+                g1_arrive(h, dirn, 1, u)
+                g1_arrive(h, dirn, 2, u)
+            for j in (0, 1):
+                lo, hi = (2, 1) if j == 0 else (1, 2)
+                for o in (2 * u, 2 * u + 1):
+                    v = (
+                        g_own[3, h, j, o].astype(F32)
+                        + recv1[h, 0, lo, o].astype(F32)
+                        + recv1[h, 1, hi, o].astype(F32)
+                    )
+                    q_sum[h, j, o] = v.astype(BF16)
+            if u == 0:
+                g2_send(h, 0, 0, 0, 0)
+                g2_send(h, 1, 0, 1, 0)
+                g2_send(h, 0, 1, 1, 1)
+            else:
+                g2_send(h, 1, 1, 0, 2)
+
+    def drain(count):
+        for cp in pending[:count]:
+            cp.wait_send()
+        del pending[:count]
+
+    own_group(0)
     zr_event(5)
-    facc = run(32, 64, fwd, facc)
+    own_group(1)
+    own_group(2)
     zr_event(6)
+    own_group(3)
+    facc = run(32, 48, fwd, facc)
+    zr_event(7)
+    facc = run(48, 64, fwd, facc)
+    zr_event(8)
+    g1_step(0)
     facc = run(64, 80, fwd, facc)
-    zr_event(7)
-    for h in (0, 1):
-        for dirn in (0, 1):
-            arrive(rt[h, dirn, 0], recv1.at[h, dirn, 0])
-            at = (1, h, 0) if dirn == 0 else (2, h, 1)
-            g_own[at] = (g_own[at].astype(F32) + recv1[h, dirn, 0].astype(F32)).astype(BF16)
-            g1_send((h, dirn, 2), g_own.at[at], plus(h) if dirn == 0 else minus(h))
-    zr_event(8)
+    zr_event(9)
+    g1_step(1)
     facc = run(80, 96, fwd, facc)
-    zr_event(9)
+    zr_event(10)
     facc = run(96, 128, fwd, facc)
-    zr_event(10)
+    zr_event(11)
     for i in range(28):
         v = seg_f[tab[3, i]] * (tab[4, i].astype(F32) * SCALE)
         hidden[:, i * BS : (i + 1) * BS] = v.astype(BF16)
-    zr_event(11)
-
-    st = {}
-
-    def g2_send(key, src, device):
-        h, dirn, n = key
-        st[key] = send(src, recv2.at[h, dirn, n], device)
-
-    for h in (0, 1):
+    zr_event(12)
+    g1_end(0)
+    zr_event(13)
+    g1_end(1)
+    drain(len(pending) - 40)
+
+    def in_part(s):
+        iu, id_ = UP.index((4, s)), DN.index((4, s))
+        for k in range(2):
+            b = s * 2 + k
+            v = own_part(z * 8 + b) + zrecv[0, iu, k].astype(F32) + zrecv[1, id_, k].astype(F32)
+            in_grad[:, b * BS : (b + 1) * BS] = v.T.astype(BF16)
+
+    def z_last(i):
         for dirn in (0, 1):
-            arrive(rt[h, dirn, 1], recv1.at[h, dirn, 1])
-            arrive(rt[h, dirn, 2], recv1.at[h, dirn, 2])
-        for j in (0, 1):
-            lo, hi = (2, 1) if j == 0 else (1, 2)
-            q_sum[h, j] = (
-                g_own[3, h, j].astype(F32)
-                + recv1[h, 0, lo].astype(F32)
-                + recv1[h, 1, hi].astype(F32)
-            ).astype(BF16)
-        g2_send((h, 0, 0), q_sum.at[h, 0, 0], plus(1 - h))
-        g2_send((h, 1, 0), q_sum.at[h, 1, 0], minus(1 - h))
-        g2_send((h, 0, 1), q_sum.at[h, 1, 1], plus(1 - h))
-        g2_send((h, 1, 1), q_sum.at[h, 0, 2], minus(1 - h))
-    zr_event(12)
-    zr_event(13)
+            arrive(zr[dirn][i], zrecv.at[dirn, i])
+
+    z_last(10)
     for h in (0, 1):
         for dirn in (0, 1):
             arrive(st[h, dirn, 0], recv2.at[h, dirn, 0])
             at = (h, 0, 1) if dirn == 0 else (h, 1, 2)
             q_sum[at] = (q_sum[at].astype(F32) + recv2[h, dirn, 0].astype(F32)).astype(BF16)
-            g2_send((h, dirn, 2), q_sum.at[at], plus(1 - h) if dirn == 0 else minus(1 - h))
-
-    for s in (2, 3, 0, 1):
-        iu, id_ = UP.index((4, s)), DN.index((4, s))
-        arrive(zr[0][iu], zrecv.at[0, iu])
-        arrive(zr[1][id_], zrecv.at[1, id_])
-        for k in range(2):
-            b = s * 2 + k
-            v = own_part(z * 8 + b) + zrecv[0, iu, k].astype(F32) + zrecv[1, id_, k].astype(F32)
-            in_grad[:, b * BS : (b + 1) * BS] = v.astype(BF16)
-
+            g2_send(h, dirn, 2, at[1], at[2])
     for tag, region in mom_t:
         arrive(tag, region)
+    z_last(11)
+    drain(len(pending) - 12)
+    z_last(12)
+    in_part(0)
+    in_part(2)
+    z_last(13)
+    in_part(1)
+    in_part(3)
+
     for h in (0, 1):
         for dirn in (0, 1):
             arrive(st[h, dirn, 1], recv2.at[h, dirn, 1])
@@ -500,7 +572,9 @@
         scratch_shapes=[
             pltpu.VMEM((64, BS, BS), BF16),
             pltpu.VMEM((BS, BS, BS), BF16),
+            pltpu.VMEM((32, BS, BS), BF16),
             pltpu.VMEM((4, 4, 2, 8, BS), I32),
+            pltpu.VMEM((28, BS, BS), BF16),
             pltpu.VMEM((28, BS, BS), BF16),
             pltpu.VMEM((3, 4, BS, BS), F32),
             pltpu.VMEM((3, 4, BS, BS), F32),

time: 61.7 us -> 59.7 us (0.968); the launches traced: 60.5 us -> 59.6 us
  Pallas kernels: 59.9 us -> 59 us
    pallas_call x1, Pallas kernels: 58.6 us -> 57.7 us  [body(): pl.pallas_call(kernel, name='step', out_shape=tuple((pltpu.VMEM(s, t) for...]
where the time goes in v3:
time: 59.7 us; the launch traced here: 59.6 us
  Pallas kernels  59 us (99%)
  between operations  0.64 us (1%)
    pallas_call x1, Pallas kernels, body(): pl.pallas_call(kernel, name='step', out_shape=tuple((pltpu.VMEM(s, t) for...  57.7 us
    pallas_call x1, Pallas kernels, body(): pl.pallas_call(store, name='store', out_shape=tuple((jax.ShapeDtypeStruct...  1.27 us

profile of v3, /device:TPU:2, one launch (start us, length us, event | category | flops | bytes accessed | tf_op | source)
XLA Modules:
  0.0 59.6 jit_solution(10506873536553059011)
XLA Ops:
  0.6 57.7 %step.1 = (bf16[4,128,128]{2,1,0:T(8,128)(2,1)S(1)}, f32[4,128,128]{2,1,0:T(8,128)S(1)}, f32[4,128,128]{2,1,0:T(8,128)S(1)}, bf16[128,3584]{1,0:T(8,128)(2,1)S(1)}, bf16[128,1024]{1,0:T(8,128)(2,1)S(1)}) custom-call(s32[4]{0:T(128)} %brow.1, s32[4]{0:T(128)} %bcol.1, s32[4]{0:T(128)} %bdst.1, bf16[4,128,128]{2,1,0:T(8,128)(2,1)} %weight.1, ...), custom_call_target="tpu_custom_call" | custom-call | tf_op jit(solution)/shard_map/step/pallas_call | solution.py:566
  58.3 1.3 %store.1 = (bf16[4,128,128]{2,1,0:T(8,128)(2,1)}, f32[4,128,128]{2,1,0:T(8,128)}, f32[4,128,128]{2,1,0:T(8,128)}, bf16[128,3584]{1,0:T(8,128)(2,1)}, bf16[128,1024]{1,0:T(8,128)(2,1)}) custom-call(bf16[4,128,128]{2,1,0:T(8,128)(2,1)S(1)} %get-tuple-element.10.a, f32[4,128,128]{2,1,0:T(8,128)S(1)} %get-tuple-element.11.b, ...), custom_call_target="tpu_custom_call" | custom-call | tf_op jit(solution)/shard_map/store/pallas_call | solution.py:601
